TPU v7x, 128 devices: a whole 4x4x4 slice. The times are simulated.
128 devices in a mesh: path: 4 (over z_lo, core), ctx: 32 (over x, z_hi, y).
Axes of the slice: x: 4, y: 4, z: 4 (z_hi: 2, z_lo: 2; z = z_hi * 2 + z_lo), core: 2. Of those that a mesh axis runs over, the one named last changes fastest.
Arguments:
- tokens: int32 [4096], P('ctx'), may hold values from 0 to 511
- sub_pos: int32 [512], P('ctx'), may hold values from 0 to 4095, as said below
- sub_base: int32 [512], P('ctx'), may hold values from 0 to 511
- embed: bfloat16 [512, 4096], replicated, may hold values from -6 to 6
- norm_gain: float32 [4096], replicated, may hold values from 0.1 to 1.9
- fir_taps: bfloat16 [3, 3, 4096], replicated, may hold values from -3.5 to 3.5
- long_filter: float32 [4096, 4096], P(None, 'ctx'), may hold values from -8 to 8
- skip_gain: float32 [4096], P('ctx'), may hold values from 0.5 to 1.5
- cotangent: bfloat16 [4096, 4096], P('ctx'), may hold values from -6 to 6
Outputs:
- path_grad: float32 [4096, 4096], P('ctx', 'path')
- attribution: float32 [4096, 4096], P('ctx', 'path')
Inputs may be any that keep to these rules, and one draw needn't show every extreme that they name: `sub_pos`: exactly one substituted position in each aligned block of 8 tokens, so the positions rise strictly.
All inputs are finite; a program needn't handle non-finite values.
Results may differ from a plain program's by a relative error of at most 0.0085.
Values may be sent and summed in bfloat16 or wider, within the bound.
A program may use at most 192 MiB of HBM per device.

v0:
```python
import jax
import jax.numpy as jnp
from jax import lax
from jax.sharding import PartitionSpec as P

PATH_DEV = 1


precise = lax.Precision.HIGH


def from_behind(block, axis, distance):
    devices = range(lax.axis_size(axis))
    route = [(i - distance, i) for i in devices if i - distance in devices]
    return lax.ppermute(block, axis, route)


def angle_tables(length):
    outer_size = 64
    inner_size = length // outer_size
    outer_idx = jnp.arange(outer_size, dtype=jnp.int32)
    inner_idx = jnp.arange(inner_size, dtype=jnp.int32)
    outer_angle = (
        2.0
        * jnp.pi
        / outer_size
        * (outer_idx[:, None] * outer_idx[None, :] % outer_size).astype(jnp.float32)
    )
    inner_angle = (
        2.0
        * jnp.pi
        / inner_size
        * (inner_idx[:, None] * inner_idx[None, :] % inner_size).astype(jnp.float32)
    )
    twist_angle = (
        2.0
        * jnp.pi
        / length
        * (outer_idx[:, None] * inner_idx[None, :] % length).astype(jnp.float32)
    )
    return (outer_angle, inner_angle, twist_angle)


def complex_table(angle, sign):
    cosine = jnp.cos(angle)
    sine = sign * jnp.sin(angle)
    return jnp.stack([jnp.stack([cosine, sine]), jnp.stack([-sine, cosine])])


def twisted(values, angle, sign):
    cosine = jnp.cos(angle)[None, :, :, None]
    sine = sign * jnp.sin(angle)[None, :, :, None]
    real_part = values[:, 0]
    imag_part = values[:, 1]
    return jnp.stack(
        [real_part * cosine - imag_part * sine, real_part * sine + imag_part * cosine], 1
    )


def spectrum(signal):
    batch, half, width = signal.shape
    length = 2 * half
    outer_angle, inner_angle, twist_angle = angle_tables(length)
    outer_size = outer_angle.shape[0]
    inner_size = inner_angle.shape[0]
    folded = signal.reshape(batch, outer_size // 2, inner_size, width)
    used = outer_angle[:, : outer_size // 2]
    outer_table = jnp.stack([jnp.cos(used), -jnp.sin(used)])
    first = jnp.einsum("rka,pabc->prkbc", outer_table, folded, precision=precise)
    turned = twisted(first, twist_angle, -1.0)
    return jnp.einsum(
        "prkbc,rsbm->pskmc", turned, complex_table(inner_angle, -1.0), precision=precise
    )


def inverse(spec):
    batch, parts, outer_size, inner_size, width = spec.shape
    length = outer_size * inner_size
    outer_angle, inner_angle, twist_angle = angle_tables(length)
    back = jnp.einsum("pskmc,stmb->ptkbc", spec, complex_table(inner_angle, 1.0), precision=precise)
    turned = twisted(back, twist_angle, 1.0)
    used = outer_angle[: outer_size // 2]
    outer_table = jnp.stack([jnp.cos(used), -jnp.sin(used)])
    result = jnp.einsum("rak,prkbc->pabc", outer_table, turned, precision=precise)
    return (result / length).reshape(batch, length // 2, width)


def long_conv(channels, filter_spec, skip_gain, adjoint):
    signal = channels.astype(jnp.float32)
    spec = spectrum(signal)
    sig_real = spec[:, 0]
    sig_imag = spec[:, 1]
    filt_real = filter_spec[:, 0]
    filt_imag = filter_spec[:, 1]
    if adjoint:
        prod_real = sig_real * filt_real + sig_imag * filt_imag
        prod_imag = sig_imag * filt_real - sig_real * filt_imag
    else:
        prod_real = sig_real * filt_real - sig_imag * filt_imag
        prod_imag = sig_real * filt_imag + sig_imag * filt_real
    return (inverse(jnp.stack([prod_real, prod_imag], 1)) + skip_gain * signal).astype(jnp.bfloat16)


def depthwise(signal, filters):
    return lax.conv_general_dilated(
        signal,
        filters[:, None, :],
        (1,),
        "VALID",
        dimension_numbers=("NWC", "WIO", "NWC"),
        feature_group_count=signal.shape[2],
        preferred_element_type=jnp.float32,
    )


def to_channels(values):
    return lax.all_to_all(values, "ctx", split_axis=2, concat_axis=1, tiled=True)


def to_tokens(values):
    return lax.all_to_all(values, "ctx", split_axis=1, concat_axis=2, tiled=True)


def body(tokens, sub_pos, sub_base, embed, norm_gain, fir_taps, long_filter, skip_gain, cotangent):
    tok_rows = tokens.shape[0]
    width = embed.shape[1]
    reach = fir_taps.shape[1] - 1
    path_size = lax.axis_size("path")
    points = PATH_DEV * path_size
    in_block = jnp.arange(8, dtype=jnp.int32)[None, :] == (sub_pos % 8)[:, None]
    base_ids = jnp.where(in_block, sub_base[:, None], tokens.reshape(-1, 8)).reshape(-1)
    emb_tok = jnp.take(embed, tokens, axis=0).astype(jnp.float32)
    emb_base = jnp.take(embed, base_ids, axis=0).astype(jnp.float32)
    difference = emb_tok - emb_base
    first_point = lax.axis_index("path") * PATH_DEV
    alphas = (
        (first_point + jnp.arange(PATH_DEV, dtype=jnp.int32)).astype(jnp.float32) + 0.5
    ) / points
    inputs = emb_base[None] + alphas[:, None, None] * difference[None]
    inv_rms = lax.rsqrt(jnp.mean(inputs * inputs, -1, keepdims=True) + 1e-06)
    normed = (inputs * inv_rms * norm_gain).astype(jnp.bfloat16)
    earlier = from_behind(normed[:, tok_rows - reach :], "ctx", 1)
    extended = jnp.concatenate([earlier, normed], 1)
    flipped = fir_taps[:, ::-1, :]
    q_feat = depthwise(extended, flipped[0])
    k_feat = depthwise(extended, flipped[1])
    v_feat = depthwise(extended, flipped[2])
    gated = (k_feat * v_feat).astype(jnp.bfloat16)
    upstream = cotangent.astype(jnp.float32)[None]
    grad_y = (upstream * q_feat).astype(jnp.bfloat16)
    filter_spec = spectrum(long_filter[None])
    conv_out = to_tokens(long_conv(to_channels(gated), filter_spec, skip_gain, False))
    grad_z = to_tokens(long_conv(to_channels(grad_y), filter_spec, skip_gain, True))
    grad_z32 = grad_z.astype(jnp.float32)
    grad_q = (upstream * conv_out.astype(jnp.float32)).astype(jnp.bfloat16)
    grad_k = (grad_z32 * v_feat).astype(jnp.bfloat16)
    grad_v = (grad_z32 * k_feat).astype(jnp.bfloat16)
    grads = (grad_q, grad_k, grad_v)
    heads = jnp.stack([grad_q[:, :reach], grad_k[:, :reach], grad_v[:, :reach]])
    later = from_behind(heads, "ctx", -1)
    grad_norm = sum(
        (
            depthwise(jnp.concatenate([grads[index], later[index]], 1), fir_taps[index])
            for index in range(3)
        )
    )
    scaled = norm_gain * grad_norm
    grad_in = inv_rms * scaled - inputs * inv_rms**3 * jnp.mean(inputs * scaled, -1, keepdims=True)
    summed = lax.psum_scatter(
        jnp.sum(grad_in, 0).astype(jnp.bfloat16), "path", scatter_dimension=1, tiled=True
    ).astype(jnp.float32)
    path_grad = summed / points
    share = width // path_size
    columns = lax.dynamic_slice_in_dim(difference, lax.axis_index("path") * share, share, 1)
    return (path_grad, columns * path_grad)


def solution(mesh):
    return jax.shard_map(
        body,
        mesh=mesh,
        in_specs=(
            P("ctx"),
            P("ctx"),
            P("ctx"),
            P(),
            P(),
            P(),
            P(None, "ctx"),
            P("ctx"),
            P("ctx", None),
        ),
        out_specs=(P("ctx", "path"), P("ctx", "path")),
        check_vma=False,
    )
```

profile of v0, /device:TPU:1, one launch (start us, length us, event | category | flops | bytes accessed | tf_op | source)
XLA Modules:
  0.0 581.1 jit_solution(8248613599338435576)
XLA Ops:
  10.4 4.9 gather_fusion
  15.3 6.3 %gather_fusion.1 = bf16[128,4096]{1,0:T(8,128)(2,1)} fusion(bf16[512,4096]{1,0:T(8,128)(2,1)} %param.14, s32[1024]{0:T(1024)S(1)} %pad_clamp_fusion), kind=kCustom, calls=%fused_computation.1.clone | custom fusion | bytes 2097664 | tf_op jit(solution)/shard_map/jit(_take)/gather | solution.py:132
  28.2 4.2 collective-permute-start
  35.8 9.5 %slice.109 = bf16[1,3,4096]{2,1,0:T(4,128)(2,1)} reverse(bf16[1,3,4096]{2,1,0:T(4,128)(2,1)S(1)} %get-tuple-element.38), dimensions={1} | reverse | bytes 49152 | tf_op jit(solution)/shard_map/slice | solution.py:147
  45.3 9.5 %slice.107 = bf16[1,3,4096]{2,1,0:T(4,128)(2,1)} reverse(bf16[1,3,4096]{2,1,0:T(4,128)(2,1)S(1)} %get-tuple-element.36), dimensions={1} | reverse | bytes 49152 | tf_op jit(solution)/shard_map/slice | solution.py:146
  54.8 9.5 %slice.124 = bf16[1,3,4096]{2,1,0:T(4,128)(2,1)} reverse(bf16[1,3,4096]{2,1,0:T(4,128)(2,1)S(1)} %get-tuple-element.37), dimensions={1} | reverse | bytes 49152 | tf_op jit(solution)/shard_map/slice | solution.py:145
  83.6 5.5 copy.169
  89.7 24.4 %reduce.3 = bf16[4096,128]{1,0:T(8,128)(2,1)} reduce(bf16[4096,1,128]{2,1,0:T(2,128)(2,1)} %bitcast.293, bf16[]{:T(256)} %broadcast.627), dimensions={1}, to_apply=%bitcast.262.reduce_sub_computation | reduce | bytes 2097154
  116.2 10.4 %all-to-all-start = ((bf16[32,2,8192]{2,1,0:T(2,128)(2,1)}), bf16[32,2,8192]{2,1,0:T(2,128)(2,1)}, u32[]{:S(2)}, u32[]{:S(2)}) async-start(bf16[32,2,8192]{2,1,0:T(2,128)(2,1)} %reshape.653), calls=%async_computation | async-start | bytes 2097152 | tf_op jit(solution)/shard_map/all_to_all | solution.py:117
  131.4 3.5 reshape.576
  135.0 3.1 slice.167
  142.8 17.0 %copy.315 = bf16[1,128,4096]{1,0,2:T(2,128)(2,1)} copy(bf16[1,128,4096]{1,2,0:T(8,128)(2,1)S(1)} %fusion.47) | data formatting | bytes 2097152 | tf_op jit(solution)/shard_map/convert_element_type | solution.py:150
  159.9 23.5 %reduce.4 = bf16[4096,128]{1,0:T(8,128)(2,1)S(1)} reduce(bf16[4096,1,128]{2,1,0:T(2,128)(2,1)} %bitcast.295, bf16[]{:T(256)} %broadcast.627), dimensions={1}, to_apply=%bitcast.282.reduce_sub_computation | reduce | bytes 2097154
  184.5 9.4 %all-to-all-start.2 = ((bf16[32,2,8192]{2,1,0:T(2,128)(2,1)}), bf16[32,2,8192]{2,1,0:T(2,128)(2,1)S(1)}, u32[]{:S(2)}, u32[]{:S(2)}) async-start(bf16[32,2,8192]{2,1,0:T(2,128)(2,1)} %reshape.649), calls=%async_computation.2 | async-start | bytes 2097152 | tf_op jit(solution)/shard_map/all_to_all | solution.py:117
  194.8 6.9 %convolution_bitcast_fusion.1 = f32[1,2,64,128,128]{4,2,1,3,0:T(8,128)} fusion(f32[32,128,128,1]{2,1,0,3:T(8,128)S(1)} %bitcast.284, f32[1,64,32]{1,2,0:T(8,128)S(1)} %get-tuple-element.49, f32[1,64,32]{1,2,0:T(8,128)S(1)} %get-tuple-element.48), kind=kOutput, calls=%fused_computation.61 | convolution fusion | flops 402657280 | bytes 10502144 | tf_op jit(solution)/shard_map/rka,pabc->prkbc/dot_general | solution.py:69
  201.8 4.3 reshape.654
  209.1 6.4 %convolution_bitcast_fusion.2 = f32[1,2,64,128,128]{4,2,1,3,0:T(8,128)} fusion(bf16[1,128,32,128]{3,2,1,0:T(8,128)(2,1)S(1)} %copy.238, f32[1,64,32]{1,2,0:T(8,128)} %copy-done.24, f32[1,64,32]{1,2,0:T(8,128)S(1)} %get-tuple-element.48), kind=kOutput, calls=%fused_computation.62 | convolution fusion | flops 402657280 | bytes 9453568 | tf_op jit(solution)/shard_map/rka,pabc->prkbc/dot_general | solution.py:69
  219.4 3.1 convolution_bitcast_fusion
  223.3 12.8 %multiply_subtract_fusion.6 = (f32[1,1,64,128,128]{4,2,1,3,0:T(8,128)}, f32[1,1,64,128,128]{4,2,1,3,0:T(8,128)}, f32[1,1,64,128,128]{4,2,1,3,0:T(8,128)}, f32[1,...) fusion(f32[1,2,64,128,128]{4,2,1,3,0:T(8,128)} %convolution_bitcast_fusion.2, ...), kind=kLoop, calls=%fused_computation.54 | loop fusion | flops 18874368 | bytes 50397184 | tf_op jit(solution)/shard_map/sub | solution.py:56
  236.1 4.1 maximum_bitcast_fusion.5
  240.2 12.2 %fusion.33 = f32[1,2,64,128,128]{4,3,2,1,0:T(8,128)S(1)} fusion(f32[2,64,128,128]{3,1,0,2:T(8,128)} %maximum_bitcast_fusion.5, f32[1,2,128,128]{2,3,0,1:T(8,128)S(1)} %get-tuple-element.40, f32[1,2,128,128]{2,3,0,1:T(8,128)S(1)} %get-tuple-element.41), kind=kOutput, calls=%fused_computation.58 | convolution fusion | flops 3221291008 | bytes 17039360 | tf_op jit(solution)/shard_map/prkbc,rsbm->pskmc/dot_general | solution.py:71
  252.4 10.1 %maximum_bitcast_fusion = (f32[2,64,128,128]{3,1,0,2:T(8,128)}, f32[2,64,128,128]{3,1,0,2:T(8,128)}) fusion(f32[1,1,64,128,128]{4,2,1,3,0:T(8,128)} %get-tuple-element.14, f32[1,1,64,128,128]{4,2,1,3,0:T(8,128)S(1)} %copy-done.9, f32[1,1,64,128,128]{4,2,1,3,0:T(8,128)} %get-tuple-element.29, f32[1,1,64,128,128]{4,2,1,3,0:T(8,128)} %get-tuple-element.30), kind=kLoop, calls=%fused_computation.2 | loop fusion | flops 4194304 | bytes 33554432 | tf_op jit(solution)/shard_map/reshape.21
  262.5 14.1 %fusion.27 = f32[1,2,64,128,128]{4,3,2,1,0:T(8,128)} fusion(f32[2,64,128,128]{3,1,0,2:T(8,128)} %get-tuple-element.58, f32[1,2,128,128]{2,3,0,1:T(8,128)S(1)} %get-tuple-element.40, f32[1,2,128,128]{2,3,0,1:T(8,128)S(1)} %get-tuple-element.41), kind=kOutput, calls=%fused_computation.56 | convolution fusion | flops 3221291008 | bytes 17039360 | tf_op jit(solution)/shard_map/prkbc,rsbm->pskmc/dot_general | solution.py:71
  276.6 13.9 %fusion.24 = f32[1,2,64,128,128]{4,3,2,1,0:T(8,128)} fusion(f32[2,64,128,128]{3,1,0,2:T(8,128)S(1)} %copy-done.2, f32[1,2,128,128]{2,3,0,1:T(8,128)S(1)} %get-tuple-element.40, f32[1,2,128,128]{2,3,0,1:T(8,128)S(1)} %get-tuple-element.41), kind=kOutput, calls=%fused_computation.55 | convolution fusion | flops 3221291008 | bytes 17039360 | tf_op jit(solution)/shard_map/prkbc,rsbm->pskmc/dot_general | solution.py:71
  290.5 11.8 %multiply_subtract_fusion.4 = (f32[1,1,64,128,128]{4,3,2,1,0:T(8,128)}, f32[1,1,64,128,128]{4,3,2,1,0:T(8,128)}, f32[1,1,64,128,128]{4,3,2,1,0:T(8,128)}, f32[1,1,64,128,128]{4,3,2,1,0:T(8,128)}) fusion(f32[1,2,64,128,128]{4,3,2,1,0:T(8,128)} %fusion.24, f32[1,2,64,128,128]{4,3,2,1,0:T(8,128)} %fusion.27, f32[1,2,64,128,128]{4,3,2,1,0:T(8,128)S(1)} %fusion.33), kind=kLoop, calls=%fused_computation.50 | loop fusion | flops 12582912 | bytes 41943040 | tf_op jit(solution)/shard_map/sub | solution.py:99
  302.4 7.0 %fusion.36 = f32[2,128,64,128]{3,1,2,0:T(8,128)S(1)} fusion(f32[1,1,64,128,128]{4,3,2,1,0:T(8,128)} %get-tuple-element.21, f32[1,1,64,128,128]{4,3,2,1,0:T(8,128)} %get-tuple-element.22, f32[1,2,128,128]{2,3,1,0:T(8,128)S(1)} %copy-done.31, f32[1,2,128,128]{2,3,1,0:T(8,128)S(1)} %copy-done.30), kind=kOutput, calls=%fused_computation.59 | convolution fusion | flops 3223388160 | bytes 17039360 | tf_op jit(solution)/shard_map/pskmc,stmb->ptkbc/dot_general | solution.py:80
  309.3 4.9 copy.312
  314.2 8.9 %fusion.30 = f32[2,128,64,128]{3,1,2,0:T(8,128)} fusion(f32[1,1,64,128,128]{4,3,2,1,0:T(8,128)} %get-tuple-element.8, f32[1,1,64,128,128]{4,3,2,1,0:T(8,128)} %get-tuple-element.7, f32[1,2,128,128]{2,3,1,0:T(8,128)S(1)} %copy-done.31, f32[1,2,128,128]{2,3,1,0:T(8,128)S(1)} %copy-done.30), kind=kOutput, calls=%fused_computation.57 | convolution fusion | flops 3223388160 | bytes 17039360 | tf_op jit(solution)/shard_map/pskmc,stmb->ptkbc/dot_general | solution.py:80
  323.1 8.3 %copy.313 = f32[2,128,64,128]{3,2,0,1:T(8,128)S(1)} copy(f32[2,128,64,128]{3,1,2,0:T(8,128)} %fusion.30) | data formatting | bytes 16777216 | tf_op jit(solution)/shard_map/pskmc,stmb->ptkbc/dot_general | solution.py:80
  331.4 6.8 %multiply_subtract_fusion.3 = (f32[1,1,64,128,128]{4,2,1,3,0:T(8,128)S(1)}, f32[1,1,64,128,128]{4,2,1,3,0:T(8,128)}, f32[1,1,64,128,128]{4,2,1,3,0:T(8,128)}, f32[1,1,64,128,128]{4,2,1,3,0:T(8,128)}) fusion(f32[1,2,64,128,128]{4,2,1,3,0:T(8,128)S(1)} %bitcast.286, f32[64,128]{0,1:T(8,128)S(1)} %copy-done.26, f32[64,128]{0,1:T(8,128)S(1)} %fusion.115, ...), kind=kLoop, calls=%fused_computation.48 | loop fusion | flops 12582912 | bytes 33619968 | tf_op jit(solution)/shard_map/sub | solution.py:56
  338.2 4.8 fusion.54
  353.2 16.7 %copy.314 = bf16[1,4096,128]{2,0,1:T(2,128)(2,1)S(1)} copy(bf16[1,4096,128]{2,1,0:T(8,128)(2,1)S(1)} %get-tuple-element.53) | data formatting | bytes 2097152 | tf_op jit(solution)/shard_map/convert_element_type | solution.py:101
  369.8 22.7 %reduce.5 = bf16[4096,128]{1,0:T(8,128)(2,1)S(1)} reduce(bf16[4096,1,128]{2,1,0:T(2,128)(2,1)S(1)} %bitcast.296, bf16[]{:T(256)} %broadcast.627), dimensions={1}, to_apply=%bitcast.281.reduce_sub_computation | reduce | bytes 2097154
  393.6 9.5 %all-to-all-start.3 = ((bf16[32,2,8192]{2,1,0:T(2,128)(2,1)}), bf16[32,2,8192]{2,1,0:T(2,128)(2,1)S(1)}, u32[]{:S(2)}, u32[]{:S(2)}) async-start(bf16[32,2,8192]{2,1,0:T(2,128)(2,1)} %reshape.651), calls=%async_computation.3 | async-start | bytes 2097152 | tf_op jit(solution)/shard_map/all_to_all | solution.py:121
  403.1 4.8 copy.198
  407.9 3.0 copy.200
  410.9 3.6 reshape.580
  417.9 3.5 reshape.578
  424.9 3.2 copy.316
  428.1 23.4 %reduce.6 = bf16[4096,128]{1,0:T(8,128)(2,1)} reduce(bf16[4096,1,128]{2,1,0:T(2,128)(2,1)S(1)} %bitcast.294, bf16[]{:T(256)} %broadcast.627), dimensions={1}, to_apply=%bitcast.283.reduce_sub_computation | reduce | bytes 2097154
  453.6 9.5 %all-to-all-start.1 = ((bf16[32,2,8192]{2,1,0:T(2,128)(2,1)}), bf16[32,2,8192]{2,1,0:T(2,128)(2,1)}, u32[]{:S(2)}, u32[]{:S(2)}) async-start(bf16[32,2,8192]{2,1,0:T(2,128)(2,1)} %reshape.655), calls=%async_computation.1 | async-start | bytes 2097152 | tf_op jit(solution)/shard_map/all_to_all | solution.py:121
  466.9 3.2 fusion.50
  471.5 5.9 %all-to-all-done.1 = bf16[32,2,8192]{2,1,0:T(2,128)(2,1)} async-done(((bf16[32,2,8192]{2,1,0:T(2,128)(2,1)}), bf16[32,2,8192]{2,1,0:T(2,128)(2,1)}, u32[]{:S(2)}, u32[]{:S(2)}) %all-to-all-start.1) | async-done | bytes 1048608 | tf_op jit(solution)/shard_map/all_to_all | solution.py:121
  477.4 4.3 reshape.656
  492.3 3.5 collective-permute-done.1
  500.3 3.8 copy.256
  536.5 3.7 reshape.574
  545.1 26.8 %reduce-scatter.2.cloned.1.call-done = bf16[128,1024]{1,0:T(8,128)(2,1)} async-done(((bf16[128,4096]{1,0:T(8,128)(2,1)}), bf16[128,1024]{1,0:T(8,128)(2,1)}) %reduce-scatter.2.cloned.1.call-update) | async-done | bytes 262160 | tf_op jit(solution)/shard_map/reduce_scatter | solution.py:169
  (215 shorter events, 133.9 us)
Async XLA Ops:
  7.2 187.6 %copy-start = (f32[4096,128]{1,0:T(8,128)S(1)}, f32[4096,128]{1,0:T(8,128)}, u32[]{:S(2)}) copy-start(f32[4096,128]{1,0:T(8,128)} %param.17) | copy-start | bytes 6291460
  10.3 13.9 %copy-start.41 = (pred[128]{0:T(512)(128)(4,1)}, pred[128]{0:T(512)(128)(4,1)S(1)}, u32[]{:S(2)}) copy-start(pred[128]{0:T(512)(128)(4,1)S(1)} %get-tuple-element.5) | copy-start | bytes 388
  10.3 13.9 %copy-start.43 = (pred[128]{0:T(512)(128)(4,1)}, pred[128]{0:T(512)(128)(4,1)S(1)}, u32[]{:S(2)}) copy-start(pred[128]{0:T(512)(128)(4,1)S(1)} %get-tuple-element.54) | copy-start | bytes 388
  15.3 9.0 %copy-start.3 = (bf16[128,4096]{1,0:T(8,128)(2,1)}, bf16[128,4096]{1,0:T(8,128)(2,1)S(1)}, u32[]{:S(2)}) copy-start(bf16[128,4096]{1,0:T(8,128)(2,1)S(1)} %gather_fusion) | copy-start | bytes 3145732
  15.3 9.0 %copy-start.39 = (f32[4096]{0:T(1024)S(1)}, f32[4096]{0:T(1024)}, u32[]{:S(2)}) copy-start(f32[4096]{0:T(1024)} %param.15) | copy-start | bytes 49156
  21.6 2.6 copy-start.5
  24.3 2.2 copy-start.45
  24.3 9.2 %copy-start.32 = (bf16[3,3,4096]{2,1,0:T(4,128)(2,1)S(1)}, bf16[3,3,4096]{2,1,0:T(4,128)(2,1)}, u32[]{:S(2)}) copy-start(bf16[3,3,4096]{2,1,0:T(4,128)(2,1)} %param.16) | copy-start | bytes 221188
  28.2 37.8 %collective-permute-start = (bf16[1,2,4096]{2,1,0:T(2,128)(2,1)}, bf16[1,2,4096]{2,1,0:T(2,128)(2,1)S(1)}, u32[]{:S(2)}, u32[]{:S(2)}) collective-permute-start(bf16[1,2,4096]{2,1,0:T(2,128)(2,1)} %slice.151), channel_id=1, source_target_pairs={{0,1},{1,2},{2,3},{3,4},{4,5},{5,6},{6,7},{7,8},{8,9},{9,10},{10,1... | collective-permute-start | bytes 49160 | tf_op jit(solution)/shard_map/ppermute | solution.py:15
  32.4 36.5 %copy-start.27 = (f32[64,64]{0,1:T(8,128)}, f32[64,64]{0,1:T(8,128)S(1)}, u32[]{:S(2)}) copy-start(f32[64,64]{0,1:T(8,128)S(1)} %fusion.113) | copy-start | bytes 49156
  34.2 160.5 %copy-start.24 = (f32[1,64,32]{1,2,0:T(8,128)}, f32[1,64,32]{1,2,0:T(8,128)S(1)}, u32[]{:S(2)}) copy-start(f32[1,64,32]{1,2,0:T(8,128)S(1)} %get-tuple-element.49) | copy-start | bytes 24580
  65.9 75.1 %copy-start.11 = (bf16[128,4096]{0,1:T(8,128)(2,1)}, bf16[128,4096]{0,1:T(8,128)(2,1)S(1)}, u32[]{:S(2)}) copy-start(bf16[128,4096]{0,1:T(8,128)(2,1)S(1)} %copy.162) | copy-start | bytes 3145732
  68.8 5.0 copy-start.49
  71.7 2.1 copy-start.38
  74.5 2.2 copy-start.17
  114.1 12.6 %copy-start.36 = (bf16[1,3,4096]{2,1,0:T(4,128)(2,1)S(1)}, bf16[1,3,4096]{2,1,0:T(4,128)(2,1)}, u32[]{:S(2)}) copy-start(bf16[1,3,4096]{2,1,0:T(4,128)(2,1)} %slice.124) | copy-start | bytes 73732
  116.2 68.3 %all-to-all-start = ((bf16[32,2,8192]{2,1,0:T(2,128)(2,1)}), bf16[32,2,8192]{2,1,0:T(2,128)(2,1)}, u32[]{:S(2)}, u32[]{:S(2)}) async-start(bf16[32,2,8192]{2,1,0:T(2,128)(2,1)} %reshape.653), calls=%async_computation | async-start | bytes 2097152 | tf_op jit(solution)/shard_map/all_to_all | solution.py:117
  184.5 32.7 %all-to-all-start.2 = ((bf16[32,2,8192]{2,1,0:T(2,128)(2,1)}), bf16[32,2,8192]{2,1,0:T(2,128)(2,1)S(1)}, u32[]{:S(2)}, u32[]{:S(2)}) async-start(bf16[32,2,8192]{2,1,0:T(2,128)(2,1)} %reshape.649), calls=%async_computation.2 | async-start | bytes 2097152 | tf_op jit(solution)/shard_map/all_to_all | solution.py:117
  194.8 6.9 %copy-start.28 = (f32[64,64]{0,1:T(8,128)S(1)}, f32[64,64]{0,1:T(8,128)}, u32[]{:S(2)}) copy-start(f32[64,64]{0,1:T(8,128)} %copy-done.27) | copy-start | bytes 49156
  240.2 12.2 %copy-start.9 = (f32[1,1,64,128,128]{4,2,1,3,0:T(8,128)S(1)}, f32[1,1,64,128,128]{4,2,1,3,0:T(8,128)}, u32[]{:S(2)}) copy-start(f32[1,1,64,128,128]{4,2,1,3,0:T(8,128)} %get-tuple-element.13) | copy-start | bytes 12582916
  262.5 14.1 %copy-start.2 = (f32[2,64,128,128]{3,1,0,2:T(8,128)S(1)}, f32[2,64,128,128]{3,1,0,2:T(8,128)}, u32[]{:S(2)}) copy-start(f32[2,64,128,128]{3,1,0,2:T(8,128)} %get-tuple-element.57) | copy-start | bytes 25165828
  290.5 11.8 %copy-start.30 = (f32[1,2,128,128]{2,3,1,0:T(8,128)S(1)}, f32[1,2,128,128]{2,3,1,0:T(8,128)}, u32[]{:S(2)}) copy-start(f32[1,2,128,128]{2,3,1,0:T(8,128)} %get-tuple-element.39) | copy-start | bytes 393220
  290.5 11.8 %copy-start.31 = (f32[1,2,128,128]{2,3,1,0:T(8,128)S(1)}, f32[1,2,128,128]{2,3,1,0:T(8,128)}, u32[]{:S(2)}) copy-start(f32[1,2,128,128]{2,3,1,0:T(8,128)} %get-tuple-element.42) | copy-start | bytes 393220
  323.1 8.3 %copy-start.26 = (f32[64,128]{0,1:T(8,128)S(1)}, f32[64,128]{0,1:T(8,128)}, u32[]{:S(2)}) copy-start(f32[64,128]{0,1:T(8,128)} %fusion.114) | copy-start | bytes 98308
  343.0 2.2 copy-start.10
  347.6 1.6 copy-start.15
  393.6 60.1 %all-to-all-start.3 = ((bf16[32,2,8192]{2,1,0:T(2,128)(2,1)}), bf16[32,2,8192]{2,1,0:T(2,128)(2,1)S(1)}, u32[]{:S(2)}, u32[]{:S(2)}) async-start(bf16[32,2,8192]{2,1,0:T(2,128)(2,1)} %reshape.651), calls=%async_computation.3 | async-start | bytes 2097152 | tf_op jit(solution)/shard_map/all_to_all | solution.py:121
  403.1 4.8 copy-start.18
  414.5 1.6 slice-start
  421.5 1.6 slice-start.1
  453.6 23.8 %all-to-all-start.1 = ((bf16[32,2,8192]{2,1,0:T(2,128)(2,1)}), bf16[32,2,8192]{2,1,0:T(2,128)(2,1)}, u32[]{:S(2)}, u32[]{:S(2)}) async-start(bf16[32,2,8192]{2,1,0:T(2,128)(2,1)} %reshape.655), calls=%async_computation.1 | async-start | bytes 2097152 | tf_op jit(solution)/shard_map/all_to_all | solution.py:121
  463.1 108.7 %reduce-scatter.2.cloned.1.call-start = ((), (), s32[]{:S(2)}) async-start(), calls=%async_computation.5 | async-start | bytes 1310720 | tf_op jit(solution)/shard_map/reduce_scatter | solution.py:169
  483.5 3.0 copy-start.12
  488.3 9.0 %copy-start.14 = (bf16[1,128,4096]{1,2,0:T(8,128)(2,1)S(1)}, bf16[1,128,4096]{1,2,0:T(8,128)(2,1)}, u32[]{:S(2)}) copy-start(bf16[1,128,4096]{1,2,0:T(8,128)(2,1)} %copy-done.13) | copy-start | bytes 3145732
  491.0 4.8 collective-permute-start.1
  527.8 2.4 copy-start.35
  527.8 2.4 copy-start.50
  530.2 1.2 copy-start.23
  531.5 1.2 copy-start.40
  536.5 3.7 copy-start.4
  536.5 3.7 copy-start.6
  536.5 3.7 copy-start.42
  536.5 3.7 copy-start.44
  540.2 2.5 copy-start.7
  540.2 2.6 copy-start.8
  540.2 2.6 copy-start.46
  540.3 2.6 copy-start.47
  542.8 31.2 %copy-start.1 = (f32[4096,128]{1,0:T(8,128)S(1)}, f32[4096,128]{1,0:T(8,128)}, u32[]{:S(2)}) copy-start(f32[4096,128]{1,0:T(8,128)} %param.17) | copy-start | bytes 6291460
  (12 other events, 12.7 us)
Sparse Core Ops, SparseCore 0:
  545.2 26.6 reduce-scatter.1
where the time goes:
time: 589 us; the launch traced here: 581 us
  local copies, waits for them, and re-layouts  221 us (38%)
  other arithmetic  179 us (30%)
  matrix products  86 us (15%)
  starting transfers between devices  44.2 us (8%)
  waiting for transfers between devices  36.3 us (6%)
  between operations  15.1 us (3%)
    unnamed x4, other arithmetic  94 us
    unnamed x123, local copies, waits for them, and re-layouts  46.4 us
    conv_general_dilated x23, local copies, waits for them, and re-layouts, depthwise(): lax.conv_general_dilated(signal, filters[:, None, :], (1,), 'VALID', dime...  42.3 us
    dot_general x3, matrix products, spectrum(): jnp.einsum('prkbc,rsbm->pskmc', turned, complex_table(inner_angle, -1.0),...  40.2 us
    reduce_scatter x1, waiting for transfers between devices, body(): lax.psum_scatter(jnp.sum(grad_in, 0).astype(jnp.bfloat16), 'path', scatte...  26.8 us
    convert_element_type x2, local copies, waits for them, and re-layouts, long_conv(): (inverse(jnp.stack([prod_real, prod_imag], 1)) + skip_gain * signal).asty...  19.8 us
    all_to_all x2, starting transfers between devices, to_channels(): lax.all_to_all(values, 'ctx', split_axis=2, concat_axis=1, tiled=True)  19.8 us
    sub x2, other arithmetic, twisted(): real_part * cosine - imag_part * sine  19.6 us
  transfers between devices with their start and end apart: 7, of which 3 were waited for; matrix products, arithmetic and copies ran while one was open for 29% of the time, Pallas kernels for 0%

commit v1 on v0

v1 whole, which is shorter than its diff:
```python
import functools

import jax
import jax.numpy as jnp
from jax import lax
from jax.experimental import pallas as pl
from jax.experimental.pallas import tpu as pltpu
from jax.sharding import PartitionSpec as P

MESH = pl.DeviceIdType.MESH
F32 = jnp.float32
BF16 = jnp.bfloat16

NP = 4
NC = 32
TB = 128
CH = 32
NB = 32
SUB = 16
VOCAB = 512
D = 4096
REACH = 2
ALPHAS = tuple((a + 0.5) / NP for a in range(NP))
VMEM_LIMIT = 60 * 1024 * 1024


def iota(shape, dim):
    return lax.broadcasted_iota(jnp.int32, shape, dim)


def rounded(x):
    return x.astype(BF16).astype(F32)


def nt_dot(a, b):
    return lax.dot_general(a, b, (((1,), (1,)), ((), ())), preferred_element_type=F32)


def gather_kernel(
    tok_ref,
    sub_pos_ref,
    sub_base_ref,
    embed_ref,
    cot_ref,
    info_ref,
    cols_ref,
    mine,
    parts,
    info_send,
    info_recv,
    cols_send,
    cols_recv,
    own_sem,
):
    path = lax.axis_index("path")
    me = lax.axis_index("ctx")

    barrier = pltpu.get_barrier_semaphore()

    @pl.loop(1, NC)
    def _(d):
        pl.semaphore_signal(
            barrier, inc=1, device_id={"ctx": lax.rem(me + d, NC)}, device_id_type=MESH
        )

    pick = (iota((CH, TB), 1) == iota((CH, TB), 0) + path * CH).astype(F32).astype(BF16)

    @pl.loop(0, NC)
    def _(j):
        block = cot_ref[:, pl.ds(pl.multiple_of(j * TB, TB), TB)]
        parts[j] = nt_dot(pick, block).astype(BF16)

    pl.semaphore_wait(barrier, NC - 1)

    def cols_copy(d, dst, slot):
        return pltpu.make_async_remote_copy(
            src_ref=parts.at[dst],
            dst_ref=cols_ref.at[slot],
            send_sem=cols_send.at[d],
            recv_sem=cols_recv.at[d],
            device_id={"ctx": dst},
            device_id_type=MESH,
        )

    def info_copy(d, dst, slot):
        return pltpu.make_async_remote_copy(
            src_ref=mine,
            dst_ref=info_ref.at[slot],
            send_sem=info_send.at[d],
            recv_sem=info_recv.at[d],
            device_id={"ctx": dst},
            device_id_type=MESH,
        )

    @pl.loop(1, NC)
    def _(d):
        cols_copy(d, lax.rem(me + d, NC), me).start()

    own_cols = pltpu.make_async_copy(parts.at[me], cols_ref.at[me], own_sem.at[0])
    own_cols.start()

    tok = tok_ref[...].astype(F32)
    diag = iota((SUB, SUB), 0) == iota((SUB, SUB), 1)
    pos_row = (sub_pos_ref[...] & 7).astype(F32)
    pos_col = jnp.sum(jnp.where(diag, pos_row, 0.0), 1, keepdims=True) + 8.0 * iota(
        (SUB, 1), 0
    ).astype(F32)
    base_col = jnp.sum(jnp.where(diag, sub_base_ref[...].astype(F32), 0.0), 1, keepdims=True)
    at_sub = iota((SUB, TB), 1).astype(F32) == pos_col
    covered = jnp.sum(jnp.where(at_sub, 1.0, 0.0), 0, keepdims=True) > 0.5
    base = jnp.where(
        covered, jnp.sum(jnp.where(at_sub, base_col, 0.0), 0, keepdims=True), tok
    )
    sub_tok_col = jnp.sum(jnp.where(at_sub, tok, 0.0), 1, keepdims=True)
    eye = iota((TB, TB), 0) == iota((TB, TB), 1)
    tok_col = jnp.sum(jnp.where(eye, tok, 0.0), 1, keepdims=True)
    ids = jnp.concatenate([tok_col, sub_tok_col, base_col], 0)
    rows = TB + 2 * SUB
    hot = (iota((rows, VOCAB), 1).astype(F32) == ids).astype(F32).astype(BF16)

    def squares(step, carry):
        plain, subs = carry
        part = embed_ref[:, pl.ds(pl.multiple_of(step * 256, 256), 256)]
        found = jnp.dot(hot, part, preferred_element_type=F32)
        own = found[:TB]
        own = own * own
        plain = plain + own[:, :TB] + own[:, TB:]
        e_tok = found[TB : TB + SUB]
        e_base = found[TB + SUB :]
        diff = e_tok - e_base
        new = []
        for a in range(NP):
            x = e_base + ALPHAS[a] * diff
            x = x * x
            new.append(subs[a] + x[:, :TB] + x[:, TB:])
        return plain, tuple(new)

    plain, subs = lax.fori_loop(
        0,
        D // 256,
        squares,
        (jnp.zeros((TB, TB), F32), tuple(jnp.zeros((SUB, TB), F32) for _ in range(NP))),
    )

    def inverse(total):
        return lax.rsqrt(jnp.sum(total, 1, keepdims=True) / D + 1e-06)

    plain_row = jnp.sum(jnp.where(eye, inverse(plain), 0.0), 0, keepdims=True)
    for a in range(NP):
        sub_row = jnp.sum(jnp.where(at_sub, inverse(subs[a]), 0.0), 0, keepdims=True)
        mine[a : a + 1, :] = jnp.where(covered, sub_row, plain_row)
    mine[4:5, :] = tok
    mine[5:6, :] = base
    mine[6:8, :] = jnp.zeros((2, TB), F32)

    @pl.loop(1, NC)
    def _(d):
        info_copy(d, lax.rem(me + d, NC), me).start()

    own_info = pltpu.make_async_copy(mine, info_ref.at[me], own_sem.at[1])
    own_info.start()

    @pl.loop(1, NC)
    def _(d):
        dst = lax.rem(me + d, NC)
        src = lax.rem(me - d + NC, NC)
        cols_copy(d, dst, src).wait_recv()
        info_copy(d, dst, src).wait_recv()
        cols_copy(d, dst, me).wait_send()
        info_copy(d, dst, me).wait_send()

    own_cols.wait()
    own_info.wait()


def gather_stage(tokens, sub_pos, sub_base, embed, cotangent):
    vmem = pl.BlockSpec(memory_space=pltpu.VMEM)
    return pl.pallas_call(
        gather_kernel,
        name="gather_stage",
        out_shape=(
            jax.ShapeDtypeStruct((NC, 8, TB), F32),
            jax.ShapeDtypeStruct((NC, CH, TB), BF16),
        ),
        in_specs=[vmem] * 5,
        out_specs=(vmem, vmem),
        scratch_shapes=[
            pltpu.VMEM((8, TB), F32),
            pltpu.VMEM((NC, CH, TB), BF16),
            pltpu.SemaphoreType.DMA((NC,)),
            pltpu.SemaphoreType.DMA((NC,)),
            pltpu.SemaphoreType.DMA((NC,)),
            pltpu.SemaphoreType.DMA((NC,)),
            pltpu.SemaphoreType.DMA((2,)),
        ],
        compiler_params=pltpu.CompilerParams(
            collective_id=0, has_side_effects=True, vmem_limit_bytes=VMEM_LIMIT
        ),
    )(tokens.reshape(1, -1), sub_pos.reshape(1, -1), sub_base.reshape(1, -1), embed, cotangent)


def take_lanes(table, index):
    rows = table.shape[0]
    low = jnp.broadcast_to(index & (TB - 1), (8, TB))
    high = jnp.broadcast_to(index >> 7, (8, TB))
    out = []
    for r in range(0, rows, 8):
        got = jnp.take_along_axis(table[r : r + 8, :TB], low, axis=1)
        for v in range(1, VOCAB // TB):
            more = jnp.take_along_axis(table[r : r + 8, v * TB : (v + 1) * TB], low, axis=1)
            got = jnp.where(high == v, more, got)
        out.append(got)
    return jnp.concatenate(out, 0)


def channel_kernel(
    path_index,
    ctx_index,
    info_ref,
    cols_ref,
    embed_ref,
    gain_ref,
    taps_ref,
    filter_ref,
    skip_ref,
    out_ref,
    ab_ref,
    emb_buf,
    table,
    taps,
    coef,
    time_filter,
    e_base_s,
    diff_s,
    key_s,
    val_s,
    stage,
    conv,
    past,
    pairs,
    toeplitz,
    acc,
    ahead,
    sem,
):
    path = path_index()
    ctx = ctx_index()
    lanes = pl.ds(pl.multiple_of(ctx * TB, TB), TB)
    load = pltpu.make_async_copy(embed_ref.at[:, lanes], emb_buf, sem)
    load.start()

    lane = iota((CH, TB), 1)
    chosen = lane == iota((CH, TB), 0) + path * CH
    pick = chosen.astype(F32).astype(BF16)

    def column(row):
        return jnp.broadcast_to(
            jnp.sum(jnp.where(chosen, row, 0.0), 1, keepdims=True), (CH, TB)
        )

    coef[0] = column(gain_ref[pl.ds(ctx, 1), :])
    coef[1] = column(skip_ref[...])
    for f in range(3):
        for j in range(3):
            taps[f * 3 + j] = column(taps_ref[f, j : j + 1, lanes].astype(F32))

    @pl.loop(0, NB)
    def _(k):
        part = filter_ref[pl.ds(pl.multiple_of(k * TB, TB), TB), :].astype(BF16)
        time_filter[k] = nt_dot(pick, part)

    load.wait()
    table[...] = nt_dot(pick, emb_buf[...])

    flip = (iota((TB, TB), 0) + iota((TB, TB), 1) == TB - 1).astype(F32).astype(BF16)
    past[...] = jnp.zeros_like(past)

    def forward(a, _):
        info = info_ref[a]
        e_tok = take_lanes(table[...], info[4:5].astype(jnp.int32))
        e_base = take_lanes(table[...], info[5:6].astype(jnp.int32))
        diff = e_tok - e_base
        e_base_s[a] = e_base
        diff_s[a] = diff
        cot = cols_ref[a].astype(F32)
        gain = coef[0]
        grads = []
        for p in range(NP):
            now = rounded((e_base + ALPHAS[p] * diff) * info[p : p + 1] * gain)
            one = pltpu.roll(now, 1, 1)
            two = pltpu.roll(now, 2, 1)
            now1 = jnp.where(lane < 1, past[p, 0], one)
            now2 = jnp.where(lane < 2, past[p, 1], two)
            past[p, 0] = one
            past[p, 1] = two
            q, k, v = (
                taps[f * 3] * now + taps[f * 3 + 1] * now1 + taps[f * 3 + 2] * now2
                for f in range(3)
            )
            key_s[a, p] = k
            val_s[a, p] = v
            stage[a, p * CH : (p + 1) * CH, :] = rounded(k * v)
            grads.append((cot * q).astype(BF16))
        turned = jnp.dot(jnp.concatenate(grads, 0), flip, preferred_element_type=F32)
        stage[NB - 1 - a, NP * CH :, :] = turned
        return 0

    lax.fori_loop(0, NB, forward, 0)

    lane8 = iota((16, TB), 1)
    sub8 = iota((16, TB), 0)

    def channel(c, _):
        rows = pl.ds(c, 8, stride=CH)
        last = jnp.zeros((8, TB), F32)
        for t in range(NB // 2):
            low = stage[2 * t, rows, :]
            high = stage[2 * t + 1, rows, :]
            pairs[16 * t : 16 * t + 16, :TB] = jnp.concatenate([low, high], 0).astype(BF16)
            pairs[16 * t : 16 * t + 16, TB:] = jnp.concatenate([last, low], 0).astype(BF16)
            last = high

        before = jnp.zeros((16, TB), F32)
        shear_before = jnp.zeros((16, TB), BF16)
        for k in range(NB):
            row = jnp.broadcast_to(time_filter[k, pl.ds(c, 1), :], (16, TB))
            turned = pltpu.roll(row, 0, 1, stride=1, stride_axis=0)
            shear = jnp.where(lane8 >= sub8, turned, before).astype(BF16)
            before = turned
            for g in range(TB // 16):
                if g == 0:
                    tile = shear
                else:
                    tile = jnp.concatenate(
                        [shear_before[:, TB - 16 * g :], shear[:, : TB - 16 * g]], 1
                    )
                toeplitz[TB * k + 16 * g : TB * k + 16 * g + 16, :] = tile
            shear_before = shear

        for s in range(NB // 2):
            size = 256 - 16 * s
            part = jnp.dot(
                pairs[:size], toeplitz[256 * s : 256 * s + 256], preferred_element_type=F32
            )
            if s == 0:
                acc[...] = part
            else:
                acc[16 * s :] += part
        for a in range(NB):
            conv[a, rows, :] = acc[8 * a : 8 * a + 8, :]
        return 0

    lax.fori_loop(0, CH, channel, 0)

    ahead[...] = jnp.zeros_like(ahead)

    def backward(step, _):
        a = NB - 1 - step
        info = info_ref[a]
        cot = cols_ref[a].astype(F32)
        e_base = e_base_s[a]
        diff = diff_s[a]
        gain = coef[0]
        skip = coef[1]
        turned = []
        for p in range(NP):
            rows = slice((NP + p) * CH, (NP + p + 1) * CH)
            turned.append(
                (conv[step, rows, :] + skip * stage[step, rows, :]).astype(BF16)
            )
        grad_z = jnp.dot(jnp.concatenate(turned, 0), flip, preferred_element_type=F32)
        total = jnp.zeros((CH, TB), F32)
        sum_a = jnp.zeros((CH, TB), F32)
        sum_b = jnp.zeros((CH, TB), F32)
        for p in range(NP):
            rows = slice(p * CH, (p + 1) * CH)
            out = rounded(conv[a, rows, :] + skip * stage[a, rows, :])
            gz = grad_z[rows]
            gq = rounded(cot * out)
            gk = rounded(gz * val_s[a, p])
            gv = rounded(gz * key_s[a, p])
            u0, u1, u2 = (taps[j] * gq + taps[3 + j] * gk + taps[6 + j] * gv for j in range(3))
            one = pltpu.roll(u1, TB - 1, 1)
            two = pltpu.roll(u2, TB - 2, 1)
            gn = (
                u0
                + jnp.where(lane < TB - 1, one, ahead[p, 0])
                + jnp.where(lane < TB - 2, two, ahead[p, 1])
            )
            ahead[p, 0] = one
            ahead[p, 1] = two
            inv = info[p : p + 1]
            scaled = gain * gn
            total = total + inv * scaled
            w = (e_base + ALPHAS[p] * diff) * scaled * (inv * inv * inv)
            sum_a = sum_a + w
            sum_b = sum_b + ALPHAS[p] * w
        out_ref[a] = total.astype(BF16)
        ab_ref[a, 0:1, :] = jnp.sum(sum_a, 0, keepdims=True)
        ab_ref[a, 1:2, :] = jnp.sum(sum_b, 0, keepdims=True)
        ab_ref[a, 2:8, :] = jnp.zeros((6, TB), F32)
        return 0

    lax.fori_loop(0, NB, backward, 0)


def axis_path():
    return lax.axis_index("path")


def axis_ctx():
    return lax.axis_index("ctx")


def channel_stage(
    info, cols, embed, gain, taps, long_filter, skip, path_index=axis_path, ctx_index=axis_ctx
):
    vmem = pl.BlockSpec(memory_space=pltpu.VMEM)
    return pl.pallas_call(
        functools.partial(channel_kernel, path_index, ctx_index),
        name="channel_stage",
        out_shape=(
            jax.ShapeDtypeStruct((NB, CH, TB), BF16),
            jax.ShapeDtypeStruct((NB, 8, TB), F32),
        ),
        in_specs=[vmem, vmem, pl.BlockSpec(memory_space=pl.ANY), vmem, vmem, vmem, vmem],
        out_specs=(vmem, vmem),
        scratch_shapes=[
            pltpu.VMEM((VOCAB, TB), BF16),
            pltpu.VMEM((CH, VOCAB), F32),
            pltpu.VMEM((9, CH, TB), F32),
            pltpu.VMEM((2, CH, TB), F32),
            pltpu.VMEM((NB, CH, TB), F32),
            pltpu.VMEM((NB, CH, TB), F32),
            pltpu.VMEM((NB, CH, TB), F32),
            pltpu.VMEM((NB, NP, CH, TB), F32),
            pltpu.VMEM((NB, NP, CH, TB), F32),
            pltpu.VMEM((NB, 2 * NP * CH, TB), F32),
            pltpu.VMEM((NB, 2 * NP * CH, TB), F32),
            pltpu.VMEM((NP, 2, CH, TB), F32),
            pltpu.VMEM((256, 256), BF16),
            pltpu.VMEM((NB * TB, TB), BF16),
            pltpu.VMEM((256, TB), F32),
            pltpu.VMEM((NP, 2, CH, TB), F32),
            pltpu.SemaphoreType.DMA,
        ],
        compiler_params=pltpu.CompilerParams(vmem_limit_bytes=VMEM_LIMIT),
    )(info, cols, embed, gain.reshape(-1, TB), taps, long_filter, skip.reshape(1, -1))


def output_kernel(
    sums_ref,
    ab_ref,
    info_ref,
    embed_ref,
    grad_ref,
    attr_ref,
    got,
    got_ab,
    group_ab,
    own_ab,
    emb_buf,
    base_s,
    diff_s,
    sums_send,
    sums_recv,
    ab_send,
    ab_recv,
    group_send,
    group_recv,
    own_sem,
):
    path = lax.axis_index("path")
    me = lax.axis_index("ctx")
    width = D // NP
    load = pltpu.make_async_copy(
        embed_ref.at[:, pl.ds(pl.multiple_of(path * width, width), width)], emb_buf, own_sem.at[2]
    )
    load.start()
    barrier = pltpu.get_barrier_semaphore()
    to_path = me // 8
    slot = (me % 8) * NP + path
    own = jnp.where(to_path == path, 1, 0)

    @pl.loop(0, NC)
    def _(s):
        src_path = lax.rem(s, NP)
        src_ctx = path * 8 + s // NP

        @pl.when((src_path != path) | (src_ctx != me))
        def _():
            pl.semaphore_signal(
                barrier,
                inc=1,
                device_id={"path": src_path, "ctx": src_ctx},
                device_id_type=MESH,
            )

    @pl.loop(1, NP)
    def _(d):
        pl.semaphore_signal(
            barrier, inc=1, device_id={"path": lax.rem(path + d, NP)}, device_id_type=MESH
        )

    pl.semaphore_wait(barrier, NC + NP - 1 - own)

    def sums_copy(dst, at, number):
        return pltpu.make_async_remote_copy(
            src_ref=sums_ref.at[dst],
            dst_ref=got.at[at],
            send_sem=sums_send.at[dst],
            recv_sem=sums_recv.at[number],
            device_id={"path": to_path, "ctx": dst},
            device_id_type=MESH,
        )

    def ab_copy(dst, at, number):
        return pltpu.make_async_remote_copy(
            src_ref=ab_ref.at[dst],
            dst_ref=got_ab.at[at],
            send_sem=ab_send.at[dst],
            recv_sem=ab_recv.at[number],
            device_id={"path": to_path, "ctx": dst},
            device_id_type=MESH,
        )

    def group_copy(d, at):
        return pltpu.make_async_remote_copy(
            src_ref=own_ab,
            dst_ref=group_ab.at[at],
            send_sem=group_send.at[d],
            recv_sem=group_recv.at[d],
            device_id={"path": lax.rem(path + d, NP)},
            device_id_type=MESH,
        )

    def is_self(dst):
        return (to_path == path) & (dst == me)

    own_sums = pltpu.make_async_copy(sums_ref.at[me], got.at[slot], own_sem.at[0])
    own_part = pltpu.make_async_copy(ab_ref.at[me], got_ab.at[slot], own_sem.at[1])

    @pl.when(to_path == path)
    def _():
        own_sums.start()
        own_part.start()

    @pl.loop(0, NC)
    def _(d):
        dst = lax.rem(me + d, NC)

        @pl.when(jnp.logical_not(is_self(dst)))
        def _():
            ab_copy(dst, slot, slot).start()
            sums_copy(dst, slot, slot).start()

    load.wait()
    info = info_ref[pl.ds(me, 1)][0]
    eye = iota((TB, TB), 0) == iota((TB, TB), 1)
    unit = eye.astype(F32).astype(BF16)

    def as_column(row):
        return jnp.sum(jnp.where(eye, row, 0.0), 1, keepdims=True)

    vocab = iota((TB, VOCAB), 1).astype(F32)
    hot_tok = (vocab == as_column(info[4:5])).astype(F32).astype(BF16)
    hot_base = (vocab == as_column(info[5:6])).astype(F32).astype(BF16)

    @pl.loop(0, width // 256)
    def _(s):
        columns = pl.ds(pl.multiple_of(s * 256, 256), 256)
        part = emb_buf[:, columns]
        e_tok = jnp.dot(hot_tok, part, preferred_element_type=F32)
        e_base = jnp.dot(hot_base, part, preferred_element_type=F32)
        base_s[:, columns] = e_base
        diff_s[:, columns] = e_tok - e_base

    self_slot = (me % 8) * NP + path

    def others(s):
        return jnp.logical_not((to_path == path) & (s == self_slot))

    @pl.loop(0, NC)
    def _(s):
        @pl.when(others(s))
        def _():
            ab_copy(me, s, s).wait_recv()

    @pl.when(to_path == path)
    def _():
        own_part.wait()

    own_ab[...] = jnp.sum(got_ab[...], 0)

    @pl.loop(1, NP)
    def _(d):
        group_copy(d, path).start()

    @pl.loop(0, NC)
    def _(s):
        @pl.when(others(s))
        def _():
            sums_copy(me, s, s).wait_recv()

    @pl.when(to_path == path)
    def _():
        own_sums.wait()

    ab = own_ab[...]
    for d in range(1, NP):
        src = lax.rem(path - d + NP, NP)
        group_copy(d, src).wait_recv()
        ab = ab + group_ab[pl.ds(src, 1)][0]
    scale = 1.0 / (NP * D)
    a_col = as_column(ab[0:1]) * scale
    b_col = as_column(ab[1:2]) * scale

    @pl.loop(0, width // TB)
    def _(s):
        columns = pl.ds(pl.multiple_of(s * TB, TB), TB)
        block = got[pl.ds(s * 4, 4)].reshape(TB, TB)
        summed = nt_dot(unit, block)
        diff = diff_s[:, columns]
        grad = summed * (1.0 / NP) - (base_s[:, columns] * a_col + diff * b_col)
        grad_ref[:, columns] = grad
        attr_ref[:, columns] = diff * grad

    @pl.loop(0, NC)
    def _(d):
        dst = lax.rem(me + d, NC)

        @pl.when(jnp.logical_not(is_self(dst)))
        def _():
            ab_copy(dst, slot, slot).wait_send()
            sums_copy(dst, slot, slot).wait_send()

    @pl.loop(1, NP)
    def _(d):
        group_copy(d, path).wait_send()


def output_stage(sums, ab, info, embed):
    vmem = pl.BlockSpec(memory_space=pltpu.VMEM)
    width = D // NP
    shape = jax.ShapeDtypeStruct((TB, width), F32)
    return pl.pallas_call(
        output_kernel,
        name="output_stage",
        out_shape=(shape, shape),
        in_specs=[vmem, vmem, vmem, pl.BlockSpec(memory_space=pl.ANY)],
        out_specs=(vmem, vmem),
        scratch_shapes=[
            pltpu.VMEM((NC, CH, TB), BF16),
            pltpu.VMEM((NC, 8, TB), F32),
            pltpu.VMEM((NP, 8, TB), F32),
            pltpu.VMEM((8, TB), F32),
            pltpu.VMEM((VOCAB, width), BF16),
            pltpu.VMEM((TB, width), F32),
            pltpu.VMEM((TB, width), F32),
            pltpu.SemaphoreType.DMA((NC,)),
            pltpu.SemaphoreType.DMA((NC,)),
            pltpu.SemaphoreType.DMA((NC,)),
            pltpu.SemaphoreType.DMA((NC,)),
            pltpu.SemaphoreType.DMA((NP,)),
            pltpu.SemaphoreType.DMA((NP,)),
            pltpu.SemaphoreType.DMA((3,)),
        ],
        compiler_params=pltpu.CompilerParams(
            collective_id=1, has_side_effects=True, vmem_limit_bytes=VMEM_LIMIT
        ),
    )(sums, ab, info, embed)


def body(tokens, sub_pos, sub_base, embed, norm_gain, fir_taps, long_filter, skip_gain, cotangent):
    info, cols = gather_stage(tokens, sub_pos, sub_base, embed, cotangent)
    sums, ab = channel_stage(info, cols, embed, norm_gain, fir_taps, long_filter, skip_gain)
    return output_stage(sums, ab, info, embed)


def solution(mesh):
    return jax.shard_map(
        body,
        mesh=mesh,
        in_specs=(
            P("ctx"),
            P("ctx"),
            P("ctx"),
            P(),
            P(),
            P(),
            P(None, "ctx"),
            P("ctx"),
            P("ctx", None),
        ),
        out_specs=(P("ctx", "path"), P("ctx", "path")),
        check_vma=False,
    )
```

time: 589 us -> 113 us (0.19); the launches traced: 581 us -> 113 us
  local copies, waits for them, and re-layouts: 221 us -> 3.77 us
  other arithmetic: 179 us -> 0 us
  Pallas kernels: 0 us -> 109 us
  matrix products: 86 us -> 0 us
  starting transfers between devices: 44.2 us -> 0 us
  waiting for transfers between devices: 36.3 us -> 0 us
  between operations: 15.1 us -> 0.65 us
    pallas_call x0 -> x3, Pallas kernels: none -> 109 us  [the longest x1 62.2 us: channel_stage(): pl.pallas_call(functools.partial(channel_kernel, path_index, ctx_index),...]
    unnamed x4 -> x0, other arithmetic: 94 us -> none
    dot_general x10 -> x0, matrix products: 79.6 us -> none  [the longest x3 40.2 us: spectrum(): jnp.einsum('prkbc,rsbm->pskmc', turned, complex_table(inner_angle, -1.0),...]
    convert_element_type x11 -> x0, local copies, waits for them, and re-layouts: 56.6 us -> none  [the longest x2 19.8 us: long_conv(): (inverse(jnp.stack([prod_real, prod_imag], 1)) + skip_gain * signal).asty...]
    unnamed x123 -> x2, local copies, waits for them, and re-layouts: 46.4 us -> 3.77 us
    conv_general_dilated x23 -> x0, local copies, waits for them, and re-layouts: 42.3 us -> none  [depthwise(): lax.conv_general_dilated(signal, filters[:, None, :], (1,), 'VALID', dime...]
    all_to_all x4 -> x0, starting transfers between devices: 38.7 us -> none  [the longest x2 19.8 us: to_channels(): lax.all_to_all(values, 'ctx', split_axis=2, concat_axis=1, tiled=True)]
    sub x3 -> x0, other arithmetic: 31.4 us -> none  [the longest x2 19.6 us: twisted(): real_part * cosine - imag_part * sine]
  transfers between devices with their start and end apart: 7 -> 0, of which waited for: 3 -> 0; matrix products, arithmetic and copies ran while one was open for 29% -> 0% of each run, Pallas kernels for 0% -> 0%
where the time goes in v1:
time: 113 us
  Pallas kernels  109 us (96%)
  local copies, waits for them, and re-layouts  3.77 us (3%)
    pallas_call x1, Pallas kernels, channel_stage(): pl.pallas_call(functools.partial(channel_kernel, path_index, ctx_index),...  62.2 us
    pallas_call x1, Pallas kernels, gather_stage(): pl.pallas_call(gather_kernel, name='gather_stage', out_shape=(jax.ShapeDt...  25 us
    pallas_call x1, Pallas kernels, output_stage(): pl.pallas_call(output_kernel, name='output_stage', out_shape=(shape, shap...  21.4 us
    unnamed x2, local copies, waits for them, and re-layouts  3.77 us

profile of v1, /device:TPU:1, one launch (start us, length us, event | category | flops | bytes accessed | tf_op | source)
XLA Modules:
  0.0 113.0 jit_solution(3123073821872916797)
XLA Ops:
  0.6 25.0 %gather_stage.1 = (f32[32,8,128]{2,1,0:T(8,128)}, bf16[32,32,128]{2,1,0:T(8,128)(2,1)}) custom-call(s32[1,128]{1,0:T(1,128)} %bitcast.6, s32[1,16]{1,0:T(1,128)} %bitcast.7, s32[1,16]{1,0:T(1,128)} %bitcast.8, bf16[512,4096]{1,0:T(8,128)(2,1)} %embed_ref.5, bf16[128,4096]{1,0:T(8,128)(2,1)} %cot_ref.1), custom_call_target="tpu_custom_call" | custom-call | tf_op jit(solution)/shard_map/gather_stage/pallas_call | solution.py:178
  25.6 62.2 %channel_stage.1 = (bf16[32,32,128]{2,1,0:T(8,128)(2,1)}, f32[32,8,128]{2,1,0:T(8,128)}) custom-call(f32[32,8,128]{2,1,0:T(8,128)} %get-tuple-element.6.info_ref, bf16[32,32,128]{2,1,0:T(8,128)(2,1)} %get-tuple-element.7.cols_ref, bf16[512,4096]{1,0:T(8,128)(2,1)} %embed_ref.5, f32[32,128]{1,0:T(8,128)} %bitcast.5, bf16[3,3,4096]{2,1,0:T(4,128)(2,1)} %taps_ref.1, ...), custom_call_target="tpu_custom_call" | custom-call | tf_op jit(solution)/shard_map/channel_stage/pallas_call | solution.py:419
  87.8 21.4 %output_stage.1 = (f32[128,1024]{1,0:T(8,128)}, f32[128,1024]{1,0:T(8,128)}) custom-call(bf16[32,32,128]{2,1,0:T(8,128)(2,1)} %get-tuple-element.8.sums_ref, f32[32,8,128]{2,1,0:T(8,128)} %get-tuple-element.9.ab_ref, f32[32,8,128]{2,1,0:T(8,128)} %get-tuple-element.6.info_ref, bf16[512,4096]{1,0:T(8,128)(2,1)} %embed_ref.5), custom_call_target="tpu_custom_call" | custom-call | tf_op jit(solution)/shard_map/output_stage/pallas_call | solution.py:646
  109.3 1.9 %copy.13 = f32[128,1024]{1,0:T(8,128)} copy(f32[128,1024]{1,0:T(8,128)} %get-tuple-element.12) | data formatting | bytes 1048576
  111.2 1.9 %copy.14 = f32[128,1024]{1,0:T(8,128)} copy(f32[128,1024]{1,0:T(8,128)} %get-tuple-element.13) | data formatting | bytes 1048576

commit v2 on v1

--- a/solution.py
+++ b/solution.py
@@ -20,6 +20,9 @@
 VOCAB = 512
 D = 4096
 REACH = 2
+STRIDE = CH + 1
+UNROLL = 1
+CHUNK = 4
 ALPHAS = tuple((a + 0.5) / NP for a in range(NP))
 VMEM_LIMIT = 60 * 1024 * 1024
 
@@ -237,9 +240,6 @@
     stage,
     conv,
     past,
-    pairs,
-    toeplitz,
-    acc,
     ahead,
     sem,
 ):
@@ -299,58 +299,78 @@
             )
             key_s[a, p] = k
             val_s[a, p] = v
-            stage[a, p * CH : (p + 1) * CH, :] = rounded(k * v)
+            stage[a, p * STRIDE : p * STRIDE + CH, :] = rounded(k * v)
             grads.append((cot * q).astype(BF16))
         turned = jnp.dot(jnp.concatenate(grads, 0), flip, preferred_element_type=F32)
-        stage[NB - 1 - a, NP * CH :, :] = turned
+        for p in range(NP):
+            at = (NP + p) * STRIDE
+            stage[NB - 1 - a, at : at + CH, :] = turned[p * CH : (p + 1) * CH]
         return 0
 
     lax.fori_loop(0, NB, forward, 0)
 
-    lane8 = iota((16, TB), 1)
-    sub8 = iota((16, TB), 0)
-
-    def channel(c, _):
-        rows = pl.ds(c, 8, stride=CH)
-        last = jnp.zeros((8, TB), F32)
-        for t in range(NB // 2):
-            low = stage[2 * t, rows, :]
-            high = stage[2 * t + 1, rows, :]
-            pairs[16 * t : 16 * t + 16, :TB] = jnp.concatenate([low, high], 0).astype(BF16)
-            pairs[16 * t : 16 * t + 16, TB:] = jnp.concatenate([last, low], 0).astype(BF16)
-            last = high
-
+    lane16 = iota((16, TB), 1)
+    sub16 = iota((16, TB), 0)
+    zero_tile = jnp.zeros((16, TB), BF16)
+
+    def channel(c):
+        rows = pl.ds(c, 8, stride=STRIDE)
+        data = [
+            jnp.concatenate([stage[2 * t, rows, :], stage[2 * t + 1, rows, :]], 0).astype(BF16)
+            for t in range(NB // 2)
+        ]
         before = jnp.zeros((16, TB), F32)
-        shear_before = jnp.zeros((16, TB), BF16)
+        rolled = [zero_tile] * 8
+        blocks = []
+        acc = None
         for k in range(NB):
             row = jnp.broadcast_to(time_filter[k, pl.ds(c, 1), :], (16, TB))
             turned = pltpu.roll(row, 0, 1, stride=1, stride_axis=0)
-            shear = jnp.where(lane8 >= sub8, turned, before).astype(BF16)
+            shear = jnp.where(lane16 >= sub16, turned, before).astype(BF16)
             before = turned
-            for g in range(TB // 16):
-                if g == 0:
-                    tile = shear
+            tiles = [shear]
+            now = [shear]
+            for g in range(1, TB // 16):
+                moved = pltpu.roll(shear, 16 * g, 1)
+                tiles.append(jnp.where(lane16 >= 16 * g, moved, rolled[g]))
+                now.append(moved)
+            rolled = now
+            blocks.append(jnp.concatenate(tiles, 0))
+            if k % (2 * CHUNK) == 2 * CHUNK - 1:
+                first = k // 2 - CHUNK + 1
+                rhs = jnp.concatenate(
+                    [
+                        jnp.concatenate([blocks[2 * n], blocks[2 * n + 1]], 1)
+                        for n in range(CHUNK)
+                    ],
+                    0,
+                )
+                blocks = []
+                lhs = jnp.concatenate(
+                    [
+                        jnp.concatenate([zero_tile] * n + data[: NB // 2 - n], 0)
+                        for n in range(CHUNK)
+                    ],
+                    1,
+                )
+                size = 256 - 16 * first
+                part = jnp.dot(lhs[:size], rhs, preferred_element_type=F32)
+                if acc is None:
+                    acc = part
                 else:
-                    tile = jnp.concatenate(
-                        [shear_before[:, TB - 16 * g :], shear[:, : TB - 16 * g]], 1
-                    )
-                toeplitz[TB * k + 16 * g : TB * k + 16 * g + 16, :] = tile
-            shear_before = shear
-
-        for s in range(NB // 2):
-            size = 256 - 16 * s
-            part = jnp.dot(
-                pairs[:size], toeplitz[256 * s : 256 * s + 256], preferred_element_type=F32
-            )
-            if s == 0:
-                acc[...] = part
-            else:
-                acc[16 * s :] += part
+                    acc = jnp.concatenate([acc[: 16 * first], acc[16 * first :] + part], 0)
         for a in range(NB):
-            conv[a, rows, :] = acc[8 * a : 8 * a + 8, :]
+            out = acc[8 * a : 8 * a + 8, :TB]
+            if a > 0:
+                out = out + acc[8 * a - 8 : 8 * a, TB:]
+            conv[a, rows, :] = out
+
+    def channels(step, _):
+        for n in range(UNROLL):
+            channel(step * UNROLL + n)
         return 0
 
-    lax.fori_loop(0, CH, channel, 0)
+    lax.fori_loop(0, CH // UNROLL, channels, 0)
 
     ahead[...] = jnp.zeros_like(ahead)
 
@@ -364,7 +384,7 @@
         skip = coef[1]
         turned = []
         for p in range(NP):
-            rows = slice((NP + p) * CH, (NP + p + 1) * CH)
+            rows = slice((NP + p) * STRIDE, (NP + p) * STRIDE + CH)
             turned.append(
                 (conv[step, rows, :] + skip * stage[step, rows, :]).astype(BF16)
             )
@@ -373,9 +393,9 @@
         sum_a = jnp.zeros((CH, TB), F32)
         sum_b = jnp.zeros((CH, TB), F32)
         for p in range(NP):
-            rows = slice(p * CH, (p + 1) * CH)
+            rows = slice(p * STRIDE, p * STRIDE + CH)
             out = rounded(conv[a, rows, :] + skip * stage[a, rows, :])
-            gz = grad_z[rows]
+            gz = grad_z[p * CH : (p + 1) * CH]
             gq = rounded(cot * out)
             gk = rounded(gz * val_s[a, p])
             gv = rounded(gz * key_s[a, p])
@@ -435,12 +455,9 @@
             pltpu.VMEM((NB, CH, TB), F32),
             pltpu.VMEM((NB, NP, CH, TB), F32),
             pltpu.VMEM((NB, NP, CH, TB), F32),
-            pltpu.VMEM((NB, 2 * NP * CH, TB), F32),
-            pltpu.VMEM((NB, 2 * NP * CH, TB), F32),
+            pltpu.VMEM((NB, 2 * NP * STRIDE, TB), F32),
+            pltpu.VMEM((NB, 2 * NP * STRIDE, TB), F32),
             pltpu.VMEM((NP, 2, CH, TB), F32),
-            pltpu.VMEM((256, 256), BF16),
-            pltpu.VMEM((NB * TB, TB), BF16),
-            pltpu.VMEM((256, TB), F32),
             pltpu.VMEM((NP, 2, CH, TB), F32),
             pltpu.SemaphoreType.DMA,
         ],

time: 113 us -> 100 us (0.88)
  Pallas kernels: 109 us -> 95.8 us
    pallas_call x1, Pallas kernels: 62.2 us -> 49.4 us  [channel_stage(): pl.pallas_call(functools.partial(channel_kernel, path_index, ctx_index),...]
where the time goes in v2:
time: 100 us
  Pallas kernels  95.8 us (96%)
  local copies, waits for them, and re-layouts  3.77 us (4%)
    pallas_call x1, Pallas kernels, channel_stage(): pl.pallas_call(functools.partial(channel_kernel, path_index, ctx_index),...  49.4 us
    pallas_call x1, Pallas kernels, gather_stage(): pl.pallas_call(gather_kernel, name='gather_stage', out_shape=(jax.ShapeDt...  25 us
    pallas_call x1, Pallas kernels, output_stage(): pl.pallas_call(output_kernel, name='output_stage', out_shape=(shape, shap...  21.4 us
    unnamed x2, local copies, waits for them, and re-layouts  3.77 us

profile of v2, /device:TPU:1, one launch (start us, length us, event | category | flops | bytes accessed | tf_op | source)
XLA Modules:
  0.0 100.2 jit_solution(7314725137235904965)
XLA Ops:
  0.6 25.0 %gather_stage.1 = (f32[32,8,128]{2,1,0:T(8,128)}, bf16[32,32,128]{2,1,0:T(8,128)(2,1)}) custom-call(s32[1,128]{1,0:T(1,128)} %bitcast.6, s32[1,16]{1,0:T(1,128)} %bitcast.7, s32[1,16]{1,0:T(1,128)} %bitcast.8, bf16[512,4096]{1,0:T(8,128)(2,1)} %embed_ref.5, bf16[128,4096]{1,0:T(8,128)(2,1)} %cot_ref.1), custom_call_target="tpu_custom_call" | custom-call | tf_op jit(solution)/shard_map/gather_stage/pallas_call | solution.py:181
  25.6 49.4 %channel_stage.1 = (bf16[32,32,128]{2,1,0:T(8,128)(2,1)}, f32[32,8,128]{2,1,0:T(8,128)}) custom-call(f32[32,8,128]{2,1,0:T(8,128)} %get-tuple-element.6.info_ref, bf16[32,32,128]{2,1,0:T(8,128)(2,1)} %get-tuple-element.7.cols_ref, bf16[512,4096]{1,0:T(8,128)(2,1)} %embed_ref.5, f32[32,128]{1,0:T(8,128)} %bitcast.5, bf16[3,3,4096]{2,1,0:T(4,128)(2,1)} %taps_ref.1, ...), custom_call_target="tpu_custom_call" | custom-call | tf_op jit(solution)/shard_map/channel_stage/pallas_call | solution.py:439
  75.0 21.4 %output_stage.1 = (f32[128,1024]{1,0:T(8,128)}, f32[128,1024]{1,0:T(8,128)}) custom-call(bf16[32,32,128]{2,1,0:T(8,128)(2,1)} %get-tuple-element.8.sums_ref, f32[32,8,128]{2,1,0:T(8,128)} %get-tuple-element.9.ab_ref, f32[32,8,128]{2,1,0:T(8,128)} %get-tuple-element.6.info_ref, bf16[512,4096]{1,0:T(8,128)(2,1)} %embed_ref.5), custom_call_target="tpu_custom_call" | custom-call | tf_op jit(solution)/shard_map/output_stage/pallas_call | solution.py:663
  96.4 1.9 %copy.13 = f32[128,1024]{1,0:T(8,128)} copy(f32[128,1024]{1,0:T(8,128)} %get-tuple-element.12) | data formatting | bytes 1048576
  98.3 1.9 %copy.14 = f32[128,1024]{1,0:T(8,128)} copy(f32[128,1024]{1,0:T(8,128)} %get-tuple-element.13) | data formatting | bytes 1048576

commit v3 on v2

v3 whole, which is shorter than its diff:
```python
import jax
import jax.numpy as jnp
from jax import lax
from jax.experimental import pallas as pl
from jax.experimental.pallas import tpu as pltpu
from jax.sharding import PartitionSpec as P

MESH = pl.DeviceIdType.MESH
F32 = jnp.float32
BF16 = jnp.bfloat16

NP = 4
NC = 32
TB = 128
CH = 32
NB = 32
SUB = 16
VOCAB = 512
D = 4096
REACH = 2
STRIDE = CH + 1
UNROLL = 1
CHUNK = 4
ALPHAS = tuple((a + 0.5) / NP for a in range(NP))
VMEM_LIMIT = 60 * 1024 * 1024


def iota(shape, dim):
    return lax.broadcasted_iota(jnp.int32, shape, dim)


def rounded(x):
    return x.astype(BF16).astype(F32)


def nt_dot(a, b):
    return lax.dot_general(a, b, (((1,), (1,)), ((), ())), preferred_element_type=F32)


def take_lanes(table, index):
    rows = table.shape[0]
    low = jnp.broadcast_to(index & (TB - 1), (8, TB))
    high = jnp.broadcast_to(index >> 7, (8, TB))
    out = []
    for r in range(0, rows, 8):
        got = jnp.take_along_axis(table[r : r + 8, :TB], low, axis=1)
        for v in range(1, VOCAB // TB):
            more = jnp.take_along_axis(table[r : r + 8, v * TB : (v + 1) * TB], low, axis=1)
            got = jnp.where(high == v, more, got)
        out.append(got)
    return jnp.concatenate(out, 0)


def fused_kernel(
    tok_ref,
    sub_pos_ref,
    sub_base_ref,
    embed_hbm,
    gain_ref,
    taps_ref,
    filter_hbm,
    skip_ref,
    cot_hbm,
    grad_ref,
    attr_ref,
    embed_ref,
    filter_ref,
    cot_ref,
    mine,
    parts,
    info_ref,
    cols_ref,
    table,
    taps,
    coef,
    time_filter,
    e_base_s,
    diff_s,
    key_s,
    val_s,
    stage,
    conv,
    past,
    ahead,
    sums,
    ab,
    got,
    got_ab,
    own_ab,
    group_ab,
    out_base,
    out_diff,
    load_sem,
    info_send,
    info_recv,
    cols_send,
    cols_recv,
    sums_send,
    sums_recv,
    ab_send,
    ab_recv,
    group_send,
    group_recv,
):
    path = lax.axis_index("path")
    me = lax.axis_index("ctx")
    width = D // NP
    to_path = me // 8
    slot = (me % 8) * NP + path
    own = jnp.where(to_path == path, 1, 0)

    load_cot = pltpu.make_async_copy(cot_hbm, cot_ref, load_sem.at[0])
    load_embed = pltpu.make_async_copy(embed_hbm, embed_ref, load_sem.at[1])
    load_filter = pltpu.make_async_copy(filter_hbm, filter_ref, load_sem.at[2])
    load_cot.start()
    load_embed.start()
    load_filter.start()

    barrier = pltpu.get_barrier_semaphore()

    @pl.loop(1, NC)
    def _(d):
        pl.semaphore_signal(
            barrier, inc=1, device_id={"ctx": lax.rem(me + d, NC)}, device_id_type=MESH
        )

    @pl.loop(0, NC)
    def _(s):
        src_path = lax.rem(s, NP)
        src_ctx = path * 8 + s // NP

        @pl.when((src_path != path) | (src_ctx != me))
        def _():
            pl.semaphore_signal(
                barrier,
                inc=1,
                device_id={"path": src_path, "ctx": src_ctx},
                device_id_type=MESH,
            )

    @pl.loop(1, NP)
    def _(d):
        pl.semaphore_signal(
            barrier, inc=1, device_id={"path": lax.rem(path + d, NP)}, device_id_type=MESH
        )

    def cols_copy(d, dst, at):
        return pltpu.make_async_remote_copy(
            src_ref=parts.at[dst],
            dst_ref=cols_ref.at[at],
            send_sem=cols_send.at[d],
            recv_sem=cols_recv.at[d],
            device_id={"ctx": dst},
            device_id_type=MESH,
        )

    def info_copy(d, dst, at):
        return pltpu.make_async_remote_copy(
            src_ref=mine,
            dst_ref=info_ref.at[at],
            send_sem=info_send.at[d],
            recv_sem=info_recv.at[d],
            device_id={"ctx": dst},
            device_id_type=MESH,
        )

    def sums_copy(dst, at, number):
        return pltpu.make_async_remote_copy(
            src_ref=sums.at[dst],
            dst_ref=got.at[at],
            send_sem=sums_send.at[dst],
            recv_sem=sums_recv.at[number],
            device_id={"path": to_path, "ctx": dst},
            device_id_type=MESH,
        )

    def ab_copy(dst, at, number):
        return pltpu.make_async_remote_copy(
            src_ref=ab.at[dst],
            dst_ref=got_ab.at[at],
            send_sem=ab_send.at[dst],
            recv_sem=ab_recv.at[number],
            device_id={"path": to_path, "ctx": dst},
            device_id_type=MESH,
        )

    def group_copy(d, at):
        return pltpu.make_async_remote_copy(
            src_ref=own_ab,
            dst_ref=group_ab.at[at],
            send_sem=group_send.at[d],
            recv_sem=group_recv.at[d],
            device_id={"path": lax.rem(path + d, NP)},
            device_id_type=MESH,
        )

    lane = iota((CH, TB), 1)
    chosen = lane == iota((CH, TB), 0) + path * CH
    pick = chosen.astype(F32).astype(BF16)
    load_cot.wait()

    @pl.loop(0, NC)
    def _(j):
        block = cot_ref[:, pl.ds(pl.multiple_of(j * TB, TB), TB)]
        parts[j] = nt_dot(pick, block).astype(BF16)

    cols_ref[pl.ds(me, 1)] = parts[pl.ds(me, 1)]

    tok = tok_ref[...].astype(F32)
    diag = iota((SUB, SUB), 0) == iota((SUB, SUB), 1)
    pos_row = (sub_pos_ref[...] & 7).astype(F32)
    pos_col = jnp.sum(jnp.where(diag, pos_row, 0.0), 1, keepdims=True) + 8.0 * iota(
        (SUB, 1), 0
    ).astype(F32)
    base_col = jnp.sum(jnp.where(diag, sub_base_ref[...].astype(F32), 0.0), 1, keepdims=True)
    at_sub = iota((SUB, TB), 1).astype(F32) == pos_col
    covered = jnp.sum(jnp.where(at_sub, 1.0, 0.0), 0, keepdims=True) > 0.5
    base = jnp.where(covered, jnp.sum(jnp.where(at_sub, base_col, 0.0), 0, keepdims=True), tok)
    sub_tok_col = jnp.sum(jnp.where(at_sub, tok, 0.0), 1, keepdims=True)
    eye = iota((TB, TB), 0) == iota((TB, TB), 1)

    def as_column(row):
        return jnp.sum(jnp.where(eye, row, 0.0), 1, keepdims=True)

    tok_col = as_column(tok)
    ids = jnp.concatenate([tok_col, sub_tok_col, base_col], 0)
    hot = (iota((TB + 2 * SUB, VOCAB), 1).astype(F32) == ids).astype(F32).astype(BF16)
    load_embed.wait()

    def squares(step, carry):
        plain, subs = carry
        part = embed_ref[:, pl.ds(pl.multiple_of(step * 256, 256), 256)]
        found = jnp.dot(hot, part, preferred_element_type=F32)
        plain_rows = found[:TB]
        plain_rows = plain_rows * plain_rows
        plain = plain + plain_rows[:, :TB] + plain_rows[:, TB:]
        e_tok = found[TB : TB + SUB]
        e_base = found[TB + SUB :]
        diff = e_tok - e_base
        new = []
        for a in range(NP):
            x = e_base + ALPHAS[a] * diff
            x = x * x
            new.append(subs[a] + x[:, :TB] + x[:, TB:])
        return plain, tuple(new)

    plain, subs = lax.fori_loop(
        0,
        D // 256,
        squares,
        (jnp.zeros((TB, TB), F32), tuple(jnp.zeros((SUB, TB), F32) for _ in range(NP))),
    )

    def inverse(total):
        return lax.rsqrt(jnp.sum(total, 1, keepdims=True) / D + 1e-06)

    plain_row = jnp.sum(jnp.where(eye, inverse(plain), 0.0), 0, keepdims=True)
    for a in range(NP):
        sub_row = jnp.sum(jnp.where(at_sub, inverse(subs[a]), 0.0), 0, keepdims=True)
        mine[a : a + 1, :] = jnp.where(covered, sub_row, plain_row)
    mine[4:5, :] = tok
    mine[5:6, :] = base
    mine[6:8, :] = jnp.zeros((2, TB), F32)
    info_ref[pl.ds(me, 1)] = mine[...].reshape(1, 8, TB)

    pl.semaphore_wait(barrier, 2 * NC + NP - 2 - own)

    @pl.loop(1, NC)
    def _(d):
        info_copy(d, lax.rem(me + d, NC), me).start()
        cols_copy(d, lax.rem(me + d, NC), me).start()

    lanes = pl.ds(pl.multiple_of(me * TB, TB), TB)

    def column(row):
        return jnp.broadcast_to(
            jnp.sum(jnp.where(chosen, row, 0.0), 1, keepdims=True), (CH, TB)
        )

    coef[0] = column(gain_ref[pl.ds(me, 1), :])
    coef[1] = column(skip_ref[...])
    for f in range(3):
        for j in range(3):
            taps[f * 3 + j] = column(taps_ref[f, j : j + 1, lanes].astype(F32))
    table[...] = nt_dot(pick, embed_ref[:, lanes])
    load_filter.wait()

    @pl.loop(0, NB)
    def _(k):
        part = filter_ref[pl.ds(pl.multiple_of(k * TB, TB), TB), :].astype(BF16)
        time_filter[k] = nt_dot(pick, part)

    vocab = iota((TB, VOCAB), 1).astype(F32)
    hot_tok = (vocab == tok_col).astype(F32).astype(BF16)
    hot_base = (vocab == as_column(base)).astype(F32).astype(BF16)

    @pl.loop(0, width // 256)
    def _(s):
        columns = pl.ds(pl.multiple_of(s * 256, 256), 256)
        part = embed_ref[:, pl.ds(pl.multiple_of(path * width + s * 256, 256), 256)]
        e_tok = jnp.dot(hot_tok, part, preferred_element_type=F32)
        e_base = jnp.dot(hot_base, part, preferred_element_type=F32)
        out_base[:, columns] = e_base
        out_diff[:, columns] = e_tok - e_base

    @pl.loop(1, NC)
    def _(d):
        dst = lax.rem(me + d, NC)
        src = lax.rem(me - d + NC, NC)
        info_copy(d, dst, src).wait_recv()
        cols_copy(d, dst, src).wait_recv()

    flip = (iota((TB, TB), 0) + iota((TB, TB), 1) == TB - 1).astype(F32).astype(BF16)
    past[...] = jnp.zeros_like(past)

    def forward(a, _):
        info = info_ref[a]
        e_tok = take_lanes(table[...], info[4:5].astype(jnp.int32))
        e_base = take_lanes(table[...], info[5:6].astype(jnp.int32))
        diff = e_tok - e_base
        e_base_s[a] = e_base
        diff_s[a] = diff
        cot = cols_ref[a].astype(F32)
        gain = coef[0]
        grads = []
        for p in range(NP):
            now = rounded((e_base + ALPHAS[p] * diff) * info[p : p + 1] * gain)
            one = pltpu.roll(now, 1, 1)
            two = pltpu.roll(now, 2, 1)
            now1 = jnp.where(lane < 1, past[p, 0], one)
            now2 = jnp.where(lane < 2, past[p, 1], two)
            past[p, 0] = one
            past[p, 1] = two
            q, k, v = (
                taps[f * 3] * now + taps[f * 3 + 1] * now1 + taps[f * 3 + 2] * now2
                for f in range(3)
            )
            key_s[a, p] = k
            val_s[a, p] = v
            stage[a, p * STRIDE : p * STRIDE + CH, :] = rounded(k * v)
            grads.append((cot * q).astype(BF16))
        turned = jnp.dot(jnp.concatenate(grads, 0), flip, preferred_element_type=F32)
        for p in range(NP):
            at = (NP + p) * STRIDE
            stage[NB - 1 - a, at : at + CH, :] = turned[p * CH : (p + 1) * CH]
        return 0

    lax.fori_loop(0, NB, forward, 0)

    lane16 = iota((16, TB), 1)
    sub16 = iota((16, TB), 0)
    zero_tile = jnp.zeros((16, TB), BF16)

    def channel(c):
        rows = pl.ds(c, 8, stride=STRIDE)
        data = [
            jnp.concatenate([stage[2 * t, rows, :], stage[2 * t + 1, rows, :]], 0).astype(BF16)
            for t in range(NB // 2)
        ]
        before = jnp.zeros((16, TB), F32)
        rolled = [zero_tile] * 8
        blocks = []
        acc = None
        for k in range(NB):
            row = jnp.broadcast_to(time_filter[k, pl.ds(c, 1), :], (16, TB))
            turned = pltpu.roll(row, 0, 1, stride=1, stride_axis=0)
            shear = jnp.where(lane16 >= sub16, turned, before).astype(BF16)
            before = turned
            tiles = [shear]
            now = [shear]
            for g in range(1, TB // 16):
                moved = pltpu.roll(shear, 16 * g, 1)
                tiles.append(jnp.where(lane16 >= 16 * g, moved, rolled[g]))
                now.append(moved)
            rolled = now
            blocks.append(jnp.concatenate(tiles, 0))
            if k % (2 * CHUNK) == 2 * CHUNK - 1:
                first = k // 2 - CHUNK + 1
                rhs = jnp.concatenate(
                    [
                        jnp.concatenate([blocks[2 * n], blocks[2 * n + 1]], 1)
                        for n in range(CHUNK)
                    ],
                    0,
                )
                blocks = []
                lhs = jnp.concatenate(
                    [
                        jnp.concatenate([zero_tile] * n + data[: NB // 2 - n], 0)
                        for n in range(CHUNK)
                    ],
                    1,
                )
                size = 256 - 16 * first
                part = jnp.dot(lhs[:size], rhs, preferred_element_type=F32)
                if acc is None:
                    acc = part
                else:
                    acc = jnp.concatenate([acc[: 16 * first], acc[16 * first :] + part], 0)
        for a in range(NB):
            out = acc[8 * a : 8 * a + 8, :TB]
            if a > 0:
                out = out + acc[8 * a - 8 : 8 * a, TB:]
            conv[a, rows, :] = out

    def channels(step, _):
        for n in range(UNROLL):
            channel(step * UNROLL + n)
        return 0

    lax.fori_loop(0, CH // UNROLL, channels, 0)

    ahead[...] = jnp.zeros_like(ahead)

    def is_self(dst):
        return (to_path == path) & (dst == me)

    def backward(step, _):
        a = lax.rem(me + 1 - step + 2 * NB, NB)
        info = info_ref[a]
        cot = cols_ref[a].astype(F32)
        e_base = e_base_s[a]
        diff = diff_s[a]
        gain = coef[0]
        skip = coef[1]
        turned = []
        for p in range(NP):
            rows = slice((NP + p) * STRIDE, (NP + p) * STRIDE + CH)
            turned.append(
                (conv[NB - 1 - a, rows, :] + skip * stage[NB - 1 - a, rows, :]).astype(BF16)
            )
        grad_z = jnp.dot(jnp.concatenate(turned, 0), flip, preferred_element_type=F32)
        total = jnp.zeros((CH, TB), F32)
        sum_a = jnp.zeros((CH, TB), F32)
        sum_b = jnp.zeros((CH, TB), F32)
        for p in range(NP):
            rows = slice(p * STRIDE, p * STRIDE + CH)
            out = rounded(conv[a, rows, :] + skip * stage[a, rows, :])
            gz = grad_z[p * CH : (p + 1) * CH]
            gq = rounded(cot * out)
            gk = rounded(gz * val_s[a, p])
            gv = rounded(gz * key_s[a, p])
            u0, u1, u2 = (taps[j] * gq + taps[3 + j] * gk + taps[6 + j] * gv for j in range(3))
            one = pltpu.roll(u1, TB - 1, 1)
            two = pltpu.roll(u2, TB - 2, 1)
            gn = (
                u0
                + jnp.where(lane < TB - 1, one, ahead[p, 0])
                + jnp.where(lane < TB - 2, two, ahead[p, 1])
            )
            ahead[p, 0] = one
            ahead[p, 1] = two
            inv = info[p : p + 1]
            scaled = gain * gn
            total = total + inv * scaled
            w = (e_base + ALPHAS[p] * diff) * scaled * (inv * inv * inv)
            sum_a = sum_a + w
            sum_b = sum_b + ALPHAS[p] * w

        @pl.when(step > 0)
        def _():
            sums[a] = total.astype(BF16)
            ab[a, 0:1, :] = jnp.sum(sum_a, 0, keepdims=True)
            ab[a, 1:2, :] = jnp.sum(sum_b, 0, keepdims=True)

            @pl.when(jnp.logical_not(is_self(a)))
            def _():
                ab_copy(a, slot, slot).start()
                sums_copy(a, slot, slot).start()

            @pl.when(is_self(a))
            def _():
                got[pl.ds(slot, 1)] = sums[pl.ds(a, 1)]
                got_ab[pl.ds(slot, 1)] = ab[pl.ds(a, 1)]

        @pl.when(a == 0)
        def _():
            ahead[...] = jnp.zeros_like(ahead)

        return 0

    lax.fori_loop(0, NB + 1, backward, 0)

    def others(s):
        return jnp.logical_not((to_path == path) & (s == slot))

    @pl.loop(0, NC)
    def _(s):
        @pl.when(others(s))
        def _():
            ab_copy(me, s, s).wait_recv()

    own_ab[...] = jnp.sum(got_ab[...], 0)

    @pl.loop(1, NP)
    def _(d):
        group_copy(d, path).start()

    @pl.loop(0, NC)
    def _(s):
        @pl.when(others(s))
        def _():
            sums_copy(me, s, s).wait_recv()

    both = own_ab[...]
    for d in range(1, NP):
        src = lax.rem(path - d + NP, NP)
        group_copy(d, src).wait_recv()
        both = both + group_ab[pl.ds(src, 1)][0]
    scale = 1.0 / (NP * D)
    a_col = as_column(both[0:1]) * scale
    b_col = as_column(both[1:2]) * scale
    unit = eye.astype(F32).astype(BF16)

    @pl.loop(0, width // TB)
    def _(s):
        columns = pl.ds(pl.multiple_of(s * TB, TB), TB)
        block = got[pl.ds(s * 4, 4)].reshape(TB, TB)
        summed = nt_dot(unit, block)
        diff = out_diff[:, columns]
        grad = summed * (1.0 / NP) - (out_base[:, columns] * a_col + diff * b_col)
        grad_ref[:, columns] = grad
        attr_ref[:, columns] = diff * grad

    @pl.loop(1, NC)
    def _(d):
        dst = lax.rem(me + d, NC)
        info_copy(d, dst, me).wait_send()
        cols_copy(d, dst, me).wait_send()

    @pl.loop(0, NC)
    def _(d):
        @pl.when(jnp.logical_not(is_self(d)))
        def _():
            ab_copy(d, slot, slot).wait_send()
            sums_copy(d, slot, slot).wait_send()

    @pl.loop(1, NP)
    def _(d):
        group_copy(d, path).wait_send()


def body(tokens, sub_pos, sub_base, embed, norm_gain, fir_taps, long_filter, skip_gain, cotangent):
    vmem = pl.BlockSpec(memory_space=pltpu.VMEM)
    here = pl.BlockSpec(memory_space=pl.ANY)
    width = D // NP
    shape = jax.ShapeDtypeStruct((TB, width), F32)
    dma = pltpu.SemaphoreType.DMA
    return pl.pallas_call(
        fused_kernel,
        name="fused_stage",
        out_shape=(shape, shape),
        in_specs=[vmem, vmem, vmem, here, vmem, vmem, here, vmem, here],
        out_specs=(vmem, vmem),
        scratch_shapes=[
            pltpu.VMEM((VOCAB, D), BF16),
            pltpu.VMEM((NB * TB, TB), F32),
            pltpu.VMEM((TB, D), BF16),
            pltpu.VMEM((8, TB), F32),
            pltpu.VMEM((NC, CH, TB), BF16),
            pltpu.VMEM((NC, 8, TB), F32),
            pltpu.VMEM((NC, CH, TB), BF16),
            pltpu.VMEM((CH, VOCAB), F32),
            pltpu.VMEM((9, CH, TB), F32),
            pltpu.VMEM((2, CH, TB), F32),
            pltpu.VMEM((NB, CH, TB), F32),
            pltpu.VMEM((NB, CH, TB), F32),
            pltpu.VMEM((NB, CH, TB), F32),
            pltpu.VMEM((NB, NP, CH, TB), F32),
            pltpu.VMEM((NB, NP, CH, TB), F32),
            pltpu.VMEM((NB, 2 * NP * STRIDE, TB), F32),
            pltpu.VMEM((NB, 2 * NP * STRIDE, TB), F32),
            pltpu.VMEM((NP, 2, CH, TB), F32),
            pltpu.VMEM((NP, 2, CH, TB), F32),
            pltpu.VMEM((NC, CH, TB), BF16),
            pltpu.VMEM((NC, 2, TB), F32),
            pltpu.VMEM((NC, CH, TB), BF16),
            pltpu.VMEM((NC, 2, TB), F32),
            pltpu.VMEM((2, TB), F32),
            pltpu.VMEM((NP, 2, TB), F32),
            pltpu.VMEM((TB, width), F32),
            pltpu.VMEM((TB, width), F32),
            dma((3,)),
            dma((NC,)),
            dma((NC,)),
            dma((NC,)),
            dma((NC,)),
            dma((NC,)),
            dma((NC,)),
            dma((NC,)),
            dma((NC,)),
            dma((NP,)),
            dma((NP,)),
        ],
        compiler_params=pltpu.CompilerParams(
            collective_id=0, has_side_effects=True, vmem_limit_bytes=VMEM_LIMIT
        ),
    )(
        tokens.reshape(1, -1),
        sub_pos.reshape(1, -1),
        sub_base.reshape(1, -1),
        embed,
        norm_gain.reshape(-1, TB),
        fir_taps,
        long_filter,
        skip_gain.reshape(1, -1),
        cotangent,
    )


def solution(mesh):
    return jax.shard_map(
        body,
        mesh=mesh,
        in_specs=(
            P("ctx"),
            P("ctx"),
            P("ctx"),
            P(),
            P(),
            P(),
            P(None, "ctx"),
            P("ctx"),
            P("ctx", None),
        ),
        out_specs=(P("ctx", "path"), P("ctx", "path")),
        check_vma=False,
    )
```

time: 100 us -> 83.5 us (0.83)
  Pallas kernels: 95.8 us -> 78.9 us
    pallas_call x3 -> x1, Pallas kernels: 95.8 us -> 78.9 us  [body(): pl.pallas_call(fused_kernel, name='fused_stage', out_shape=(shape, shape)...]
where the time goes in v3:
time: 83.5 us; the launch traced here: 83.3 us
  Pallas kernels  78.9 us (94%)
  local copies, waits for them, and re-layouts  3.77 us (5%)
    pallas_call x1, Pallas kernels, body(): pl.pallas_call(fused_kernel, name='fused_stage', out_shape=(shape, shape)...  78.9 us
    unnamed x2, local copies, waits for them, and re-layouts  3.77 us

profile of v3, /device:TPU:1, one launch (start us, length us, event | category | flops | bytes accessed | tf_op | source)
XLA Modules:
  0.0 83.3 jit_solution(15851575196531344837)
XLA Ops:
  0.6 78.9 %fused_stage.1 = (f32[128,1024]{1,0:T(8,128)}, f32[128,1024]{1,0:T(8,128)}) custom-call(s32[1,128]{1,0:T(1,128)} %bitcast.6, s32[1,16]{1,0:T(1,128)} %bitcast.7, s32[1,16]{1,0:T(1,128)} %bitcast.8, bf16[512,4096]{1,0:T(8,128)(2,1)} %embed_hbm.1, f32[32,128]{1,0:T(8,128)} %bitcast.5, bf16[3,3,4096]{2,1,0:T(4,128)(2,1)} %taps_ref.1, f32[4096,128]{1,0:T(8,128)} %filter_hbm.1, ...), custom_call_target="tpu_custom_call" | custom-call | tf_op jit(solution)/shard_map/fused_stage/pallas_call | solution.py:549
  79.5 1.9 %copy.13 = f32[128,1024]{1,0:T(8,128)} copy(f32[128,1024]{1,0:T(8,128)} %get-tuple-element.4) | data formatting | bytes 1048576
  81.4 1.9 %copy.14 = f32[128,1024]{1,0:T(8,128)} copy(f32[128,1024]{1,0:T(8,128)} %get-tuple-element.5) | data formatting | bytes 1048576

commit v4 on v3

--- a/solution.py
+++ b/solution.py
@@ -20,7 +20,9 @@
 REACH = 2
 STRIDE = CH + 1
 UNROLL = 1
-CHUNK = 4
+CHUNK = 2
+FLIPS = 4
+OUT = 512
 ALPHAS = tuple((a + 0.5) / NP for a in range(NP))
 VMEM_LIMIT = 60 * 1024 * 1024
 
@@ -61,8 +63,10 @@
     filter_hbm,
     skip_ref,
     cot_hbm,
-    grad_ref,
-    attr_ref,
+    sums_out,
+    both_out,
+    tok_out,
+    base_out,
     embed_ref,
     filter_ref,
     cot_ref,
@@ -88,8 +92,8 @@
     got_ab,
     own_ab,
     group_ab,
-    out_base,
-    out_diff,
+    turn,
+    grad_z,
     load_sem,
     info_send,
     info_recv,
@@ -109,6 +113,9 @@
     slot = (me % 8) * NP + path
     own = jnp.where(to_path == path, 1, 0)
 
+    def partner(ctx):
+        return jnp.where(ctx // 4 % 2 == me // 4 % 2, path, lax.rem(path + 2, NP))
+
     load_cot = pltpu.make_async_copy(cot_hbm, cot_ref, load_sem.at[0])
     load_embed = pltpu.make_async_copy(embed_hbm, embed_ref, load_sem.at[1])
     load_filter = pltpu.make_async_copy(filter_hbm, filter_ref, load_sem.at[2])
@@ -120,8 +127,12 @@
 
     @pl.loop(1, NC)
     def _(d):
+        other = lax.rem(me + d, NC)
         pl.semaphore_signal(
-            barrier, inc=1, device_id={"ctx": lax.rem(me + d, NC)}, device_id_type=MESH
+            barrier,
+            inc=1,
+            device_id={"path": partner(other), "ctx": other},
+            device_id_type=MESH,
         )
 
     @pl.loop(0, NC)
@@ -150,7 +161,7 @@
             dst_ref=cols_ref.at[at],
             send_sem=cols_send.at[d],
             recv_sem=cols_recv.at[d],
-            device_id={"ctx": dst},
+            device_id={"path": partner(dst), "ctx": dst},
             device_id_type=MESH,
         )
 
@@ -160,7 +171,7 @@
             dst_ref=info_ref.at[at],
             send_sem=info_send.at[d],
             recv_sem=info_recv.at[d],
-            device_id={"ctx": dst},
+            device_id={"path": partner(dst), "ctx": dst},
             device_id_type=MESH,
         )
 
@@ -199,10 +210,13 @@
     pick = chosen.astype(F32).astype(BF16)
     load_cot.wait()
 
-    @pl.loop(0, NC)
-    def _(j):
-        block = cot_ref[:, pl.ds(pl.multiple_of(j * TB, TB), TB)]
-        parts[j] = nt_dot(pick, block).astype(BF16)
+    @pl.loop(0, NC // 4)
+    def _(step):
+        to = partner(4 * step)
+        want = (lane == iota((CH, TB), 0) + to * CH).astype(F32).astype(BF16)
+        for n in range(4):
+            block = cot_ref[:, pl.ds(pl.multiple_of((4 * step + n) * TB, TB), TB)]
+            parts[4 * step + n] = nt_dot(want, block).astype(BF16)
 
     cols_ref[pl.ds(me, 1)] = parts[pl.ds(me, 1)]
 
@@ -285,10 +299,13 @@
     table[...] = nt_dot(pick, embed_ref[:, lanes])
     load_filter.wait()
 
-    @pl.loop(0, NB)
+    @pl.loop(0, NB // 8)
     def _(k):
-        part = filter_ref[pl.ds(pl.multiple_of(k * TB, TB), TB), :].astype(BF16)
-        time_filter[k] = nt_dot(pick, part)
+        for n in range(2):
+            at = pl.multiple_of(k * 8 * TB + n * 4 * TB, 4 * TB)
+            rows = nt_dot(pick, filter_ref[pl.ds(at, 4 * TB), :].astype(BF16))
+            for m in range(4):
+                time_filter[8 * k + 4 * n + m] = rows[:, m * TB : (m + 1) * TB]
 
     vocab = iota((TB, VOCAB), 1).astype(F32)
     hot_tok = (vocab == tok_col).astype(F32).astype(BF16)
@@ -300,8 +317,8 @@
         part = embed_ref[:, pl.ds(pl.multiple_of(path * width + s * 256, 256), 256)]
         e_tok = jnp.dot(hot_tok, part, preferred_element_type=F32)
         e_base = jnp.dot(hot_base, part, preferred_element_type=F32)
-        out_base[:, columns] = e_base
-        out_diff[:, columns] = e_tok - e_base
+        tok_out[:, columns] = e_tok.astype(BF16)
+        base_out[:, columns] = e_base.astype(BF16)
 
     @pl.loop(1, NC)
     def _(d):
@@ -322,7 +339,6 @@
         diff_s[a] = diff
         cot = cols_ref[a].astype(F32)
         gain = coef[0]
-        grads = []
         for p in range(NP):
             now = rounded((e_base + ALPHAS[p] * diff) * info[p : p + 1] * gain)
             one = pltpu.roll(now, 1, 1)
@@ -338,14 +354,26 @@
             key_s[a, p] = k
             val_s[a, p] = v
             stage[a, p * STRIDE : p * STRIDE + CH, :] = rounded(k * v)
-            grads.append((cot * q).astype(BF16))
-        turned = jnp.dot(jnp.concatenate(grads, 0), flip, preferred_element_type=F32)
-        for p in range(NP):
-            at = (NP + p) * STRIDE
-            stage[NB - 1 - a, at : at + CH, :] = turned[p * CH : (p + 1) * CH]
+            turn[a, p * CH : (p + 1) * CH, :] = (cot * q).astype(BF16)
         return 0
 
-    lax.fori_loop(0, NB, forward, 0)
+    def forward_pair(step, _):
+        forward(2 * step, 0)
+        forward(2 * step + 1, 0)
+        return 0
+
+    lax.fori_loop(0, NB // 2, forward_pair, 0)
+
+    def flip_in(step, _):
+        for n in range(FLIPS):
+            a = step * FLIPS + n
+            turned = jnp.dot(turn[a], flip, preferred_element_type=F32)
+            for p in range(NP):
+                at = (NP + p) * STRIDE
+                stage[NB - 1 - a, at : at + CH, :] = turned[p * CH : (p + 1) * CH]
+        return 0
+
+    lax.fori_loop(0, NB // FLIPS, flip_in, 0)
 
     lane16 = iota((16, TB), 1)
     sub16 = iota((16, TB), 0)
@@ -397,6 +425,7 @@
                     acc = part
                 else:
                     acc = jnp.concatenate([acc[: 16 * first], acc[16 * first :] + part], 0)
+                yield
         for a in range(NB):
             out = acc[8 * a : 8 * a + 8, :TB]
             if a > 0:
@@ -404,13 +433,28 @@
             conv[a, rows, :] = out
 
     def channels(step, _):
-        for n in range(UNROLL):
-            channel(step * UNROLL + n)
+        running = [channel(step * UNROLL + n) for n in range(UNROLL)]
+        while running:
+            running = [x for x in running if next(x, "end") is None]
         return 0
 
     lax.fori_loop(0, CH // UNROLL, channels, 0)
 
     ahead[...] = jnp.zeros_like(ahead)
+
+    def flip_out(step, _):
+        for n in range(FLIPS):
+            a = step * FLIPS + n
+            got_rows = []
+            for p in range(NP):
+                rows = slice((NP + p) * STRIDE, (NP + p) * STRIDE + CH)
+                got_rows.append((conv[a, rows, :] + coef[1] * stage[a, rows, :]).astype(BF16))
+            grad_z[NB - 1 - a] = jnp.dot(
+                jnp.concatenate(got_rows, 0), flip, preferred_element_type=F32
+            )
+        return 0
+
+    lax.fori_loop(0, NB // FLIPS, flip_out, 0)
 
     def is_self(dst):
         return (to_path == path) & (dst == me)
@@ -423,20 +467,13 @@
         diff = diff_s[a]
         gain = coef[0]
         skip = coef[1]
-        turned = []
-        for p in range(NP):
-            rows = slice((NP + p) * STRIDE, (NP + p) * STRIDE + CH)
-            turned.append(
-                (conv[NB - 1 - a, rows, :] + skip * stage[NB - 1 - a, rows, :]).astype(BF16)
-            )
-        grad_z = jnp.dot(jnp.concatenate(turned, 0), flip, preferred_element_type=F32)
         total = jnp.zeros((CH, TB), F32)
         sum_a = jnp.zeros((CH, TB), F32)
         sum_b = jnp.zeros((CH, TB), F32)
         for p in range(NP):
             rows = slice(p * STRIDE, p * STRIDE + CH)
             out = rounded(conv[a, rows, :] + skip * stage[a, rows, :])
-            gz = grad_z[p * CH : (p + 1) * CH]
+            gz = grad_z[a, p * CH : (p + 1) * CH, :]
             gq = rounded(cot * out)
             gk = rounded(gz * val_s[a, p])
             gv = rounded(gz * key_s[a, p])
@@ -507,20 +544,8 @@
         src = lax.rem(path - d + NP, NP)
         group_copy(d, src).wait_recv()
         both = both + group_ab[pl.ds(src, 1)][0]
-    scale = 1.0 / (NP * D)
-    a_col = as_column(both[0:1]) * scale
-    b_col = as_column(both[1:2]) * scale
-    unit = eye.astype(F32).astype(BF16)
-
-    @pl.loop(0, width // TB)
-    def _(s):
-        columns = pl.ds(pl.multiple_of(s * TB, TB), TB)
-        block = got[pl.ds(s * 4, 4)].reshape(TB, TB)
-        summed = nt_dot(unit, block)
-        diff = out_diff[:, columns]
-        grad = summed * (1.0 / NP) - (out_base[:, columns] * a_col + diff * b_col)
-        grad_ref[:, columns] = grad
-        attr_ref[:, columns] = diff * grad
+    both_out[...] = both
+    sums_out[...] = got[...]
 
     @pl.loop(1, NC)
     def _(d):
@@ -540,18 +565,43 @@
         group_copy(d, path).wait_send()
 
 
+def output_kernel(sums_ref, both_ref, tok_ref, base_ref, grad_ref, attr_ref):
+    eye = iota((TB, TB), 0) == iota((TB, TB), 1)
+    unit = eye.astype(F32).astype(BF16)
+    scale = 1.0 / (NP * D)
+
+    def as_column(row):
+        return jnp.sum(jnp.where(eye, row, 0.0), 1, keepdims=True) * scale
+
+    a_col = as_column(both_ref[0:1])
+    b_col = as_column(both_ref[1:2])
+    for n in range(OUT // TB):
+        columns = slice(n * TB, (n + 1) * TB)
+        summed = nt_dot(unit, sums_ref[4 * n : 4 * n + 4].reshape(TB, TB))
+        e_base = base_ref[:, columns].astype(F32)
+        diff = tok_ref[:, columns].astype(F32) - e_base
+        grad = summed * (1.0 / NP) - (e_base * a_col + diff * b_col)
+        grad_ref[:, columns] = grad
+        attr_ref[:, columns] = diff * grad
+
+
 def body(tokens, sub_pos, sub_base, embed, norm_gain, fir_taps, long_filter, skip_gain, cotangent):
     vmem = pl.BlockSpec(memory_space=pltpu.VMEM)
     here = pl.BlockSpec(memory_space=pl.ANY)
     width = D // NP
-    shape = jax.ShapeDtypeStruct((TB, width), F32)
+    rows = jax.ShapeDtypeStruct((TB, width), BF16)
     dma = pltpu.SemaphoreType.DMA
-    return pl.pallas_call(
+    sums, both, e_tok, e_base = pl.pallas_call(
         fused_kernel,
         name="fused_stage",
-        out_shape=(shape, shape),
+        out_shape=(
+            jax.ShapeDtypeStruct((NC, CH, TB), BF16),
+            jax.ShapeDtypeStruct((2, TB), F32),
+            rows,
+            rows,
+        ),
         in_specs=[vmem, vmem, vmem, here, vmem, vmem, here, vmem, here],
-        out_specs=(vmem, vmem),
+        out_specs=(vmem, vmem, vmem, vmem),
         scratch_shapes=[
             pltpu.VMEM((VOCAB, D), BF16),
             pltpu.VMEM((NB * TB, TB), F32),
@@ -578,8 +628,8 @@
             pltpu.VMEM((NC, 2, TB), F32),
             pltpu.VMEM((2, TB), F32),
             pltpu.VMEM((NP, 2, TB), F32),
-            pltpu.VMEM((TB, width), F32),
-            pltpu.VMEM((TB, width), F32),
+            pltpu.VMEM((NB, NP * CH, TB), BF16),
+            pltpu.VMEM((NB, NP * CH, TB), F32),
             dma((3,)),
             dma((NC,)),
             dma((NC,)),
@@ -606,6 +656,21 @@
         skip_gain.reshape(1, -1),
         cotangent,
     )
+    block = pl.BlockSpec((TB, OUT), lambda i: (0, i))
+    shape = jax.ShapeDtypeStruct((TB, width), F32)
+    return pl.pallas_call(
+        output_kernel,
+        name="output_stage",
+        grid=(width // OUT,),
+        out_shape=(shape, shape),
+        in_specs=[
+            pl.BlockSpec((OUT // CH, CH, TB), lambda i: (i, 0, 0)),
+            pl.BlockSpec((2, TB), lambda i: (0, 0)),
+            block,
+            block,
+        ],
+        out_specs=(block, block),
+    )(sums, both, e_tok, e_base)
 
 
 def solution(mesh):

time: 83.5 us -> 69.7 us (0.83)
  Pallas kernels: 78.9 us -> 68.9 us
  local copies, waits for them, and re-layouts: 3.77 us -> 0 us
    pallas_call x1 -> x2, Pallas kernels: 78.9 us -> 68.9 us  [the longest x1 66.6 us: body(): pl.pallas_call(fused_kernel, name='fused_stage', out_shape=(jax.ShapeDtyp...]
    unnamed x2 -> x0, local copies, waits for them, and re-layouts: 3.77 us -> none
where the time goes in v4:
time: 69.7 us; the launch traced here: 69.5 us
  Pallas kernels  68.9 us (99%)
    pallas_call x1, Pallas kernels, body(): pl.pallas_call(fused_kernel, name='fused_stage', out_shape=(jax.ShapeDtyp...  66.6 us
    pallas_call x1, Pallas kernels, body(): pl.pallas_call(output_kernel, name='output_stage', grid=(width // OUT,),...  2.3 us

profile of v4, /device:TPU:1, one launch (start us, length us, event | category | flops | bytes accessed | tf_op | source)
XLA Modules:
  0.0 69.5 jit_solution(4147868115518340888)
XLA Ops:
  0.6 66.6 %fused_stage.1 = (bf16[32,32,128]{2,1,0:T(8,128)(2,1)}, f32[2,128]{1,0:T(2,128)}, bf16[128,1024]{1,0:T(8,128)(2,1)}, bf16[128,1024]{1,0:T(8,128)(2,1)}) custom-call(s32[1,128]{1,0:T(1,128)} %bitcast.6, s32[1,16]{1,0:T(1,128)} %bitcast.7, s32[1,16]{1,0:T(1,128)} %bitcast.8, bf16[512,4096]{1,0:T(8,128)(2,1)} %embed_hbm.1, f32[32,128]{1,0:T(8,128)} %bitcast.5, ...), custom_call_target="tpu_custom_call" | custom-call | tf_op jit(solution)/shard_map/fused_stage/pallas_call | solution.py:594
  67.2 2.3 %output_stage.1 = (f32[128,1024]{1,0:T(8,128)}, f32[128,1024]{1,0:T(8,128)}) custom-call(bf16[32,32,128]{2,1,0:T(8,128)(2,1)} %get-tuple-element.6.sums_ref, f32[2,128]{1,0:T(2,128)} %get-tuple-element.7.both_ref, bf16[128,1024]{1,0:T(8,128)(2,1)} %get-tuple-element.8.tok_ref, bf16[128,1024]{1,0:T(8,128)(2,1)} %get-tuple-element.9.base_ref), custom_call_target="tpu_custom_call" | custom-call | tf_op jit(solution)/shard_map/output_stage/pallas_call | solution.py:661

commit v5 on v4

--- a/solution.py
+++ b/solution.py
@@ -94,6 +94,7 @@
     group_ab,
     turn,
     grad_z,
+    shears,
     load_sem,
     info_send,
     info_recv,
@@ -319,6 +320,22 @@
         e_base = jnp.dot(hot_base, part, preferred_element_type=F32)
         tok_out[:, columns] = e_tok.astype(BF16)
         base_out[:, columns] = e_base.astype(BF16)
+
+    lane16 = iota((16, TB), 1)
+    sub16 = iota((16, TB), 0)
+
+    def shear_channel(c, _):
+        before = jnp.zeros((16, TB), F32)
+        for k in range(NB):
+            row = jnp.broadcast_to(time_filter[k, pl.ds(c, 1), :], (16, TB))
+            turned = pltpu.roll(row, 0, 1, stride=1, stride_axis=0)
+            shears[c, 16 * k : 16 * k + 16, :] = jnp.where(
+                lane16 >= sub16, turned, before
+            ).astype(BF16)
+            before = turned
+        return 0
+
+    lax.fori_loop(0, CH, shear_channel, 0)
 
     @pl.loop(1, NC)
     def _(d):
@@ -375,67 +392,85 @@
 
     lax.fori_loop(0, NB // FLIPS, flip_in, 0)
 
-    lane16 = iota((16, TB), 1)
-    sub16 = iota((16, TB), 0)
+    low16 = lane16 < TB // 2
+    low8 = iota((8, TB), 1) < TB // 2
     zero_tile = jnp.zeros((16, TB), BF16)
 
     def channel(c):
         rows = pl.ds(c, 8, stride=STRIDE)
-        data = [
-            jnp.concatenate([stage[2 * t, rows, :], stage[2 * t + 1, rows, :]], 0).astype(BF16)
-            for t in range(NB // 2)
-        ]
-        before = jnp.zeros((16, TB), F32)
-        rolled = [zero_tile] * 8
+        even, odd = [], []
+        data = turned_data = zero_tile
+        for t in range(NB // 2):
+            tile = jnp.concatenate(
+                [stage[2 * t, rows, :], stage[2 * t + 1, rows, :]], 0
+            ).astype(BF16)
+            swapped = pltpu.roll(tile, TB // 2, 1)
+            even.append(jnp.where(low16, tile, turned_data))
+            odd.append(jnp.where(low16, swapped, data))
+            data, turned_data = tile, swapped
+        rolled = [zero_tile] * 4
         blocks = []
         acc = None
         for k in range(NB):
-            row = jnp.broadcast_to(time_filter[k, pl.ds(c, 1), :], (16, TB))
-            turned = pltpu.roll(row, 0, 1, stride=1, stride_axis=0)
-            shear = jnp.where(lane16 >= sub16, turned, before).astype(BF16)
-            before = turned
+            shear = shears[c, 16 * k : 16 * k + 16, :]
             tiles = [shear]
             now = [shear]
-            for g in range(1, TB // 16):
+            for g in range(1, 4):
                 moved = pltpu.roll(shear, 16 * g, 1)
                 tiles.append(jnp.where(lane16 >= 16 * g, moved, rolled[g]))
                 now.append(moved)
             rolled = now
             blocks.append(jnp.concatenate(tiles, 0))
-            if k % (2 * CHUNK) == 2 * CHUNK - 1:
-                first = k // 2 - CHUNK + 1
+            if k % (4 * CHUNK) == 4 * CHUNK - 1:
+                first = k // 4 - CHUNK + 1
                 rhs = jnp.concatenate(
                     [
                         jnp.concatenate([blocks[2 * n], blocks[2 * n + 1]], 1)
-                        for n in range(CHUNK)
+                        for n in range(2 * CHUNK)
                     ],
                     0,
                 )
                 blocks = []
+                count = NB // 2 - 2 * first
                 lhs = jnp.concatenate(
                     [
-                        jnp.concatenate([zero_tile] * n + data[: NB // 2 - n], 0)
+                        jnp.concatenate(
+                            ([zero_tile] * (2 * n) + even)[:count]
+                            + ([zero_tile] * (2 * n) + odd)[:count],
+                            0,
+                        )
                         for n in range(CHUNK)
                     ],
                     1,
                 )
-                size = 256 - 16 * first
-                part = jnp.dot(lhs[:size], rhs, preferred_element_type=F32)
+                part = jnp.dot(lhs, rhs, preferred_element_type=F32)
                 if acc is None:
                     acc = part
                 else:
-                    acc = jnp.concatenate([acc[: 16 * first], acc[16 * first :] + part], 0)
-                yield
+                    skip_rows = 32 * first
+                    acc = jnp.concatenate(
+                        [
+                            acc[:skip_rows],
+                            acc[skip_rows:256] + part[: 16 * count],
+                            acc[256 : 256 + skip_rows],
+                            acc[256 + skip_rows :] + part[16 * count :],
+                        ],
+                        0,
+                    )
+        last = jnp.zeros((8, TB), F32)
         for a in range(NB):
             out = acc[8 * a : 8 * a + 8, :TB]
+            side = acc[256 + 8 * a : 264 + 8 * a, :TB]
             if a > 0:
                 out = out + acc[8 * a - 8 : 8 * a, TB:]
-            conv[a, rows, :] = out
+                side = side + acc[248 + 8 * a : 256 + 8 * a, TB:]
+            swapped = pltpu.roll(side, TB // 2, 1)
+            conv[a, rows, :] = out + jnp.where(low8, last, swapped)
+            last = swapped
 
     def channels(step, _):
-        running = [channel(step * UNROLL + n) for n in range(UNROLL)]
-        while running:
-            running = [x for x in running if next(x, "end") is None]
+        for n in range(UNROLL):
+            channel(step * UNROLL + n)
         return 0
 
     lax.fori_loop(0, CH // UNROLL, channels, 0)
@@ -630,6 +665,7 @@
             pltpu.VMEM((NP, 2, TB), F32),
             pltpu.VMEM((NB, NP * CH, TB), BF16),
             pltpu.VMEM((NB, NP * CH, TB), F32),
+            pltpu.VMEM((CH, NB * 16, TB), BF16),
             dma((3,)),
             dma((NC,)),
             dma((NC,)),

time: 69.7 us -> 64.5 us (0.925)
  Pallas kernels: 68.9 us -> 63.7 us
    pallas_call x1, Pallas kernels: 66.6 us -> 61.4 us  [body(): pl.pallas_call(fused_kernel, name='fused_stage', out_shape=(jax.ShapeDtyp...]
where the time goes in v5:
time: 64.5 us; the launch traced here: 64.4 us
  Pallas kernels  63.7 us (99%)
    pallas_call x1, Pallas kernels, body(): pl.pallas_call(fused_kernel, name='fused_stage', out_shape=(jax.ShapeDtyp...  61.4 us
    pallas_call x1, Pallas kernels, body(): pl.pallas_call(output_kernel, name='output_stage', grid=(width // OUT,),...  2.3 us

profile of v5, /device:TPU:1, one launch (start us, length us, event | category | flops | bytes accessed | tf_op | source)
XLA Modules:
  0.0 64.4 jit_solution(11865644123155629904)
XLA Ops:
  0.6 61.4 %fused_stage.1 = (bf16[32,32,128]{2,1,0:T(8,128)(2,1)}, f32[2,128]{1,0:T(2,128)}, bf16[128,1024]{1,0:T(8,128)(2,1)}, bf16[128,1024]{1,0:T(8,128)(2,1)}) custom-call(s32[1,128]{1,0:T(1,128)} %bitcast.6, s32[1,16]{1,0:T(1,128)} %bitcast.7, s32[1,16]{1,0:T(1,128)} %bitcast.8, bf16[512,4096]{1,0:T(8,128)(2,1)} %embed_hbm.1, f32[32,128]{1,0:T(8,128)} %bitcast.5, ...), custom_call_target="tpu_custom_call" | custom-call | tf_op jit(solution)/shard_map/fused_stage/pallas_call | solution.py:629
  62.1 2.3 %output_stage.1 = (f32[128,1024]{1,0:T(8,128)}, f32[128,1024]{1,0:T(8,128)}) custom-call(bf16[32,32,128]{2,1,0:T(8,128)(2,1)} %get-tuple-element.6.sums_ref, f32[2,128]{1,0:T(2,128)} %get-tuple-element.7.both_ref, bf16[128,1024]{1,0:T(8,128)(2,1)} %get-tuple-element.8.tok_ref, bf16[128,1024]{1,0:T(8,128)(2,1)} %get-tuple-element.9.base_ref), custom_call_target="tpu_custom_call" | custom-call | tf_op jit(solution)/shard_map/output_stage/pallas_call | solution.py:697

commit v6 on v5

--- a/solution.py
+++ b/solution.py
@@ -19,9 +19,9 @@
 D = 4096
 REACH = 2
 STRIDE = CH + 1
-UNROLL = 1
+UNROLL = 8
 CHUNK = 2
-FLIPS = 4
+FLIPS = 8
 OUT = 512
 ALPHAS = tuple((a + 0.5) / NP for a in range(NP))
 VMEM_LIMIT = 60 * 1024 * 1024
@@ -244,24 +244,26 @@
 
     def squares(step, carry):
         plain, subs = carry
-        part = embed_ref[:, pl.ds(pl.multiple_of(step * 256, 256), 256)]
-        found = jnp.dot(hot, part, preferred_element_type=F32)
-        plain_rows = found[:TB]
-        plain_rows = plain_rows * plain_rows
-        plain = plain + plain_rows[:, :TB] + plain_rows[:, TB:]
-        e_tok = found[TB : TB + SUB]
-        e_base = found[TB + SUB :]
-        diff = e_tok - e_base
-        new = []
-        for a in range(NP):
-            x = e_base + ALPHAS[a] * diff
-            x = x * x
-            new.append(subs[a] + x[:, :TB] + x[:, TB:])
-        return plain, tuple(new)
+        for n in range(2):
+            part = embed_ref[:, pl.ds(pl.multiple_of(step * 512 + n * 256, 256), 256)]
+            found = jnp.dot(hot, part, preferred_element_type=F32)
+            plain_rows = found[:TB]
+            plain_rows = plain_rows * plain_rows
+            plain = plain + (plain_rows[:, :TB] + plain_rows[:, TB:])
+            e_tok = found[TB : TB + SUB]
+            e_base = found[TB + SUB :]
+            diff = e_tok - e_base
+            new = []
+            for a in range(NP):
+                x = e_base + ALPHAS[a] * diff
+                x = x * x
+                new.append(subs[a] + (x[:, :TB] + x[:, TB:]))
+            subs = tuple(new)
+        return plain, subs
 
     plain, subs = lax.fori_loop(
         0,
-        D // 256,
+        D // 512,
         squares,
         (jnp.zeros((TB, TB), F32), tuple(jnp.zeros((SUB, TB), F32) for _ in range(NP))),
     )

time: 64.5 us -> 54.5 us (0.84)
  Pallas kernels: 63.7 us -> 53.7 us
    pallas_call x1, Pallas kernels: 61.4 us -> 51.4 us  [body(): pl.pallas_call(fused_kernel, name='fused_stage', out_shape=(jax.ShapeDtyp...]
where the time goes in v6:
time: 54.5 us; the launch traced here: 54.3 us
  Pallas kernels  53.7 us (99%)
  between operations  0.64 us (1%)
    pallas_call x1, Pallas kernels, body(): pl.pallas_call(fused_kernel, name='fused_stage', out_shape=(jax.ShapeDtyp...  51.4 us
    pallas_call x1, Pallas kernels, body(): pl.pallas_call(output_kernel, name='output_stage', grid=(width // OUT,),...  2.3 us

profile of v6, /device:TPU:1, one launch (start us, length us, event | category | flops | bytes accessed | tf_op | source)
XLA Modules:
  0.0 54.3 jit_solution(7730521728308283216)
XLA Ops:
  0.6 51.4 %fused_stage.1 = (bf16[32,32,128]{2,1,0:T(8,128)(2,1)}, f32[2,128]{1,0:T(2,128)}, bf16[128,1024]{1,0:T(8,128)(2,1)}, bf16[128,1024]{1,0:T(8,128)(2,1)}) custom-call(s32[1,128]{1,0:T(1,128)} %bitcast.6, s32[1,16]{1,0:T(1,128)} %bitcast.7, s32[1,16]{1,0:T(1,128)} %bitcast.8, bf16[512,4096]{1,0:T(8,128)(2,1)} %embed_hbm.1, f32[32,128]{1,0:T(8,128)} %bitcast.5, ...), custom_call_target="tpu_custom_call" | custom-call | tf_op jit(solution)/shard_map/fused_stage/pallas_call | solution.py:631
  52.0 2.3 %output_stage.1 = (f32[128,1024]{1,0:T(8,128)}, f32[128,1024]{1,0:T(8,128)}) custom-call(bf16[32,32,128]{2,1,0:T(8,128)(2,1)} %get-tuple-element.6.sums_ref, f32[2,128]{1,0:T(2,128)} %get-tuple-element.7.both_ref, bf16[128,1024]{1,0:T(8,128)(2,1)} %get-tuple-element.8.tok_ref, bf16[128,1024]{1,0:T(8,128)(2,1)} %get-tuple-element.9.base_ref), custom_call_target="tpu_custom_call" | custom-call | tf_op jit(solution)/shard_map/output_stage/pallas_call | solution.py:699

commit v7 on v6

--- a/solution.py
+++ b/solution.py
@@ -376,12 +376,12 @@
             turn[a, p * CH : (p + 1) * CH, :] = (cot * q).astype(BF16)
         return 0
 
-    def forward_pair(step, _):
-        forward(2 * step, 0)
-        forward(2 * step + 1, 0)
+    def forward_blocks(step, _):
+        for n in range(4):
+            forward(4 * step + n, 0)
         return 0
 
-    lax.fori_loop(0, NB // 2, forward_pair, 0)
+    lax.fori_loop(0, NB // 4, forward_blocks, 0)
 
     def flip_in(step, _):
         for n in range(FLIPS):

time: 54.5 us -> 53.6 us (0.983)
  Pallas kernels: 53.7 us -> 52.7 us
    pallas_call x1, Pallas kernels: 51.4 us -> 50.5 us  [body(): pl.pallas_call(fused_kernel, name='fused_stage', out_shape=(jax.ShapeDtyp...]
where the time goes in v7:
time: 53.6 us; the launch traced here: 53.4 us
  Pallas kernels  52.7 us (98%)
  between operations  0.64 us (1%)
    pallas_call x1, Pallas kernels, body(): pl.pallas_call(fused_kernel, name='fused_stage', out_shape=(jax.ShapeDtyp...  50.5 us
    pallas_call x1, Pallas kernels, body(): pl.pallas_call(output_kernel, name='output_stage', grid=(width // OUT,),...  2.3 us

profile of v7, /device:TPU:1, one launch (start us, length us, event | category | flops | bytes accessed | tf_op | source)
XLA Modules:
  0.0 53.4 jit_solution(15230579558633674062)
XLA Ops:
  0.6 50.5 %fused_stage.1 = (bf16[32,32,128]{2,1,0:T(8,128)(2,1)}, f32[2,128]{1,0:T(2,128)}, bf16[128,1024]{1,0:T(8,128)(2,1)}, bf16[128,1024]{1,0:T(8,128)(2,1)}) custom-call(s32[1,128]{1,0:T(1,128)} %bitcast.6, s32[1,16]{1,0:T(1,128)} %bitcast.7, s32[1,16]{1,0:T(1,128)} %bitcast.8, bf16[512,4096]{1,0:T(8,128)(2,1)} %embed_hbm.1, f32[32,128]{1,0:T(8,128)} %bitcast.5, ...), custom_call_target="tpu_custom_call" | custom-call | tf_op jit(solution)/shard_map/fused_stage/pallas_call | solution.py:631
  51.1 2.3 %output_stage.1 = (f32[128,1024]{1,0:T(8,128)}, f32[128,1024]{1,0:T(8,128)}) custom-call(bf16[32,32,128]{2,1,0:T(8,128)(2,1)} %get-tuple-element.6.sums_ref, f32[2,128]{1,0:T(2,128)} %get-tuple-element.7.both_ref, bf16[128,1024]{1,0:T(8,128)(2,1)} %get-tuple-element.8.tok_ref, bf16[128,1024]{1,0:T(8,128)(2,1)} %get-tuple-element.9.base_ref), custom_call_target="tpu_custom_call" | custom-call | tf_op jit(solution)/shard_map/output_stage/pallas_call | solution.py:699
